TPU v7x, 32 devices: a whole 2x2x4 slice. The times are simulated.
32 devices in a mesh: sweep: 2 (over x), cx: 4 (over z), cy: 4 (over y, core).
Axes of the slice: x: 2, y: 2, z: 4, core: 2. Of those that a mesh axis runs over, the one named last changes fastest.
Arguments:
- right_side: float32 [2, 320, 32, 512], P('sweep', None, 'cx', 'cy'), may hold values from -6 to 6
- inverse_table: bfloat16 [4, 320, 320], replicated, may hold values from -1 to 3
- coupling_table: bfloat16 [2, 6, 80, 320], replicated, may hold values from -0.3125 to 0.3125
- block_kind: int32 [2, 32, 512], P('sweep', 'cx', 'cy'), may hold values from 0 to 3
- face_kind: int32 [2, 6, 32, 512], P('sweep', None, 'cx', 'cy'), may hold values from 0 to 1
Outputs:
- solution: float32 [2, 320, 32, 512], P('sweep', None, 'cx', 'cy')
All inputs are finite; a program needn't handle non-finite values.
Results may differ from a plain program's by a relative error of at most 0.0095.
Values may be sent and summed in bfloat16 or wider, within the bound.
A program may use at most 64 MiB of HBM per device.

v0:
```python
import jax
import jax.numpy as jnp
from jax import lax
from jax.sharding import PartitionSpec as P

NVAR = 5
NP = 4
BLOCK = 320
TRACE = 80
KD = 4
KC = 2
SWEEPS = 2


def extended(cells, sides, width):
    for axis, dim in sides:
        count = lax.axis_size(axis)
        ends = count - 1
        head = lax.slice_in_dim(cells, 0, width, axis=dim)
        tail = lax.slice_in_dim(cells, cells.shape[dim] - width, cells.shape[dim], axis=dim)
        cells = jnp.concatenate(
            [
                lax.ppermute(tail, axis, [(i, (i + 1) % count) for i in range(ends)]),
                cells,
                lax.ppermute(head, axis, [((i + 1) % count, i) for i in range(ends)]),
            ],
            axis=dim,
        )
    return cells


def passed_along(value, axis, steps):
    count = lax.axis_size(axis)
    initial, last = (max(0, -steps), min(count, count - steps))
    return lax.ppermute(value, axis, [(source, source + steps) for source in range(initial, last)])


def sweep_trace(block_values, high_side):
    columns = block_values.shape[-1]
    node_view = block_values.reshape(NVAR, NP, NP * NP, columns)
    picked = node_view[:, NP - 1] if high_side else node_view[:, 0]
    return picked.reshape(TRACE, columns).astype(jnp.bfloat16)


def wide_coupling(coupling_table, face_list):
    chosen = jnp.stack([coupling_table[:, face_index] for face_index in face_list], axis=1)
    return jnp.transpose(chosen, (3, 1, 0, 2)).reshape(BLOCK, len(face_list) * KC * TRACE)


def coupling_product(incoming, face_mask, coupling_wide):
    stacked = jnp.where(face_mask[:, :, None, :], incoming[:, None], jnp.zeros((), jnp.bfloat16))
    return jnp.dot(
        coupling_wide, stacked.reshape(-1, incoming.shape[-1]), preferred_element_type=jnp.float32
    )


def inverse_product(residual, kind_mask, inverse_wide):
    stacked = jnp.where(kind_mask[:, None, :], residual[None], jnp.zeros((), jnp.bfloat16))
    return jnp.dot(
        inverse_wide,
        stacked.reshape(KD * BLOCK, residual.shape[-1]),
        preferred_element_type=jnp.float32,
    )


def start_traces(iterate, width_x, width_y):
    planes = iterate.shape[0]
    cell_count = width_x * width_y
    node_view = iterate.reshape(planes, NVAR, NP, NP, NP, width_x, width_y)

    def shaped(member):
        return member.reshape(planes, TRACE, width_x, width_y).astype(jnp.bfloat16)

    sweep_low = shaped(node_view[:, :, 0])
    sweep_high = shaped(node_view[:, :, NP - 1])
    low_x = shaped(node_view[:, :, :, 0])
    high_x = shaped(node_view[:, :, :, NP - 1])
    low_y = shaped(node_view[:, :, :, :, 0])
    high_y = shaped(node_view[:, :, :, :, NP - 1])
    rims_x = jnp.stack([low_x[:, :, 0], high_x[:, :, width_x - 1]], axis=2)
    padded_x = extended(rims_x, (("cx", 2),), 1)
    from_xlow = jnp.concatenate([padded_x[:, :, 0:1], high_x[:, :, :-1]], axis=2)
    from_xhigh = jnp.concatenate([low_x[:, :, 1:], padded_x[:, :, 3:4]], axis=2)
    rims_y = jnp.stack([low_y[:, :, :, 0], high_y[:, :, :, width_y - 1]], axis=3)
    padded_y = extended(rims_y, (("cy", 3),), 1)
    from_ylow = jnp.concatenate([padded_y[:, :, :, 0:1], high_y[:, :, :, :-1]], axis=3)
    from_yhigh = jnp.concatenate([low_y[:, :, :, 1:], padded_y[:, :, :, 3:4]], axis=3)
    return [
        member.reshape(planes, TRACE, cell_count)
        for member in (sweep_low, sweep_high, from_xlow, from_xhigh, from_ylow, from_yhigh)
    ]


def shards(right_side, inverse_table, coupling_table, block_kind, face_kind):
    planes, _, width_x, width_y = right_side.shape
    cell_count = width_x * width_y
    devices = lax.axis_size("sweep")
    position = lax.axis_index("sweep")
    rhs_flat = right_side.reshape(planes, BLOCK, cell_count)
    kind_mask = block_kind.reshape(planes, 1, cell_count) == jnp.arange(
        KD, dtype=jnp.int32
    ).reshape(1, KD, 1)
    face_mask = face_kind.reshape(planes, 6, 1, cell_count) == jnp.arange(
        KC, dtype=jnp.int32
    ).reshape(1, 1, KC, 1)
    inverse_wide = jnp.transpose(inverse_table, (1, 0, 2)).reshape(BLOCK, KD * BLOCK)
    group_count = 2
    group_width = cell_count // group_count

    def run_half(iterate, carried_faces, first_half, forward):
        if first_half:
            empty_faces = jnp.zeros((planes, TRACE, cell_count), jnp.bfloat16)
            sweep_low, sweep_high, from_xlow, from_xhigh, from_ylow, from_yhigh = (
                empty_faces,
                empty_faces,
                empty_faces,
                empty_faces,
                empty_faces,
                empty_faces,
            )
        else:
            sweep_low, sweep_high, from_xlow, from_xhigh, from_ylow, from_yhigh = start_traces(
                iterate, width_x, width_y
            )
        if forward:
            other_side = jnp.concatenate([sweep_low[1:], carried_faces[None]], axis=0)
            chain_face = 0
            other_face = 1
        else:
            other_side = jnp.concatenate([carried_faces[None], sweep_high[:-1]], axis=0)
            chain_face = 1
            other_face = 0
        fixed_traces = jnp.stack([other_side, from_xlow, from_xhigh, from_ylow, from_yhigh], axis=1)
        fixed_faces = (other_face, 2, 3, 4, 5)
        fixed_wide = wide_coupling(coupling_table, fixed_faces)
        chain_wide = wide_coupling(coupling_table, (chain_face,))
        fixed_mask = jnp.stack([face_mask[:, face_index] for face_index in fixed_faces], axis=1)
        chain_mask = face_mask[:, chain_face : chain_face + 1]

        def fixed_part(plane_index, offset, span_width):
            rhs_part = lax.dynamic_slice_in_dim(rhs_flat[plane_index], offset, span_width, 1)
            if first_half:
                return rhs_part
            traces_part = lax.dynamic_slice_in_dim(fixed_traces[plane_index], offset, span_width, 2)
            mask_part = lax.dynamic_slice_in_dim(fixed_mask[plane_index], offset, span_width, 2)
            return rhs_part - coupling_product(traces_part, mask_part, fixed_wide)

        def base_part(plane_index, offset):
            return fixed_part(plane_index, offset, group_width)

        def section_work(section_index, carried):
            current, outgoing, received_all = carried
            if forward:
                arrived = passed_along(outgoing, "sweep", 1)
                group_index = section_index - position
            else:
                arrived = passed_along(outgoing, "sweep", -1)
                group_index = section_index - (devices - 1 - position)
            active = jnp.logical_and(group_index >= 0, group_index < group_count)
            offset = jnp.clip(group_index, 0, group_count - 1) * group_width

            def compute(operands):
                current_in, received_in = operands
                front_trace = arrived
                ordering = range(planes) if forward else range(planes - 1, -1, -1)
                for plane_index in ordering:
                    kinds_part = lax.dynamic_slice_in_dim(
                        kind_mask[plane_index], offset, group_width, 1
                    )
                    chain_part = lax.dynamic_slice_in_dim(
                        chain_mask[plane_index], offset, group_width, 2
                    )
                    residual = (
                        base_part(plane_index, offset)
                        - coupling_product(front_trace[None], chain_part, chain_wide)
                    ).astype(jnp.bfloat16)
                    updated = inverse_product(residual, kinds_part, inverse_wide)
                    current_in = lax.dynamic_update_slice(
                        current_in, updated[None], (jnp.int32(plane_index), jnp.int32(0), offset)
                    )
                    front_trace = sweep_trace(updated, forward)
                received_in = lax.dynamic_update_slice_in_dim(received_in, arrived, offset, 1)
                return (current_in, received_in, front_trace)

            def skip_group(operands):
                current_in, received_in = operands
                return (current_in, received_in, jnp.zeros_like(outgoing))

            current, received_all, outgoing = lax.cond(
                active, compute, skip_group, (current, received_all)
            )
            return (current, outgoing, received_all)

        initial = (
            iterate,
            jnp.zeros((TRACE, group_width), jnp.bfloat16),
            jnp.zeros((TRACE, cell_count), jnp.bfloat16),
        )
        iterate, _, received_all = lax.fori_loop(
            0, group_count + devices - 1, section_work, initial
        )
        return (iterate, received_all)

    iterate = jnp.zeros((planes, BLOCK, cell_count), jnp.float32)
    carried_faces = jnp.zeros((TRACE, cell_count), jnp.bfloat16)
    for sweep_index in range(SWEEPS):
        iterate, carried_faces = run_half(iterate, carried_faces, sweep_index == 0, True)
        iterate, carried_faces = run_half(iterate, carried_faces, False, False)
    return iterate.reshape(planes, BLOCK, width_x, width_y)


def solution(mesh):
    in_specs = (
        P("sweep", None, "cx", "cy"),
        P(),
        P(),
        P("sweep", "cx", "cy"),
        P("sweep", None, "cx", "cy"),
    )
    out_specs = P("sweep", None, "cx", "cy")
    return jax.shard_map(shards, mesh=mesh, in_specs=in_specs, out_specs=out_specs, check_vma=False)
```

profile of v0, /device:TPU:0, one launch (start us, length us, event | category | flops | bytes accessed | tf_op | source)
XLA Modules:
  0.0 245.4 jit_solution(17791116879502238380)
XLA Ops:
  7.4 24.9 %while.77 = (s32[]{:T(128)}, f32[1,320,1024]{2,1,0:T(8,128)S(1)}, bf16[80,512]{1,0:T(8,128)(2,1)}, bf16[80,1024]{1,0:T(8,128)(2,1)}, s32[]{:T(128)}, /*index=5*/...) while((s32[]{:T(128)}, f32[1,320,1024]{2,1,0:T(8,128)S(1)}, ...), condition=%wide.region_3.4_spmd.clone, body=%wide.region_0.3_spmd.clone.sunk | while | flops 473090048 | bytes 11281909 | solution.py:199
  7.4 4.8 %collective-permute-start = (bf16[80,512]{1,0:T(8,128)(2,1)}, bf16[80,512]{1,0:T(8,128)(2,1)S(1)}, u32[]{:S(2)}, u32[]{:S(2)}) collective-permute-start(bf16[80,512]{1,0:T(8,128)(2,1)} %get-tuple-element.1949), channel_id=1, source_target_pairs={{0,16},{1,17},{2,18},{3,19},{4,20},{5,21},{6,22},{7,23},{8,24},{9,... | collective-permute-start | bytes 245768 | tf_op jit(solution)/shard_map/while/body/eval_jaxpr/ppermute | solution.py:35
  12.3 2.3 collective-permute-done
  14.6 3.3 %conditional.12 = (f32[1,320,1024]{2,1,0:T(8,128)S(1)}, bf16[80,1024]{1,0:T(8,128)(2,1)}, bf16[80,512]{1,0:T(8,128)(2,1)}) conditional(s32[]{:T(128)} %convert_element_type.236, (f32[1,320,1024]{2,1,0:T(8,128)S(1)}, bf16[80,1024]{1,0:T(8,128)(2,1)}) %tuple.210, (s32[]{:T(128)}, s32[1024]{0:T(1024)S(1)}, f32[1,320,8,128]{3,2,1,0:T(8,128)S(1)}, ...), branch_computations={%region_1.1_spmd, %region_2.2_spmd} | conditional | flops 473090048 | bytes 10937546 | solution.py:189
  19.4 2.3 collective-permute-done
  21.8 3.3 %conditional.12 = (f32[1,320,1024]{2,1,0:T(8,128)S(1)}, bf16[80,1024]{1,0:T(8,128)(2,1)}, bf16[80,512]{1,0:T(8,128)(2,1)}) conditional(s32[]{:T(128)} %convert_element_type.236, (f32[1,320,1024]{2,1,0:T(8,128)S(1)}, bf16[80,1024]{1,0:T(8,128)(2,1)}) %tuple.210, (s32[]{:T(128)}, s32[1024]{0:T(1024)S(1)}, f32[1,320,8,128]{3,2,1,0:T(8,128)S(1)}, ...), branch_computations={%region_1.1_spmd, %region_2.2_spmd} | conditional | flops 473090048 | bytes 10937546 | solution.py:189
  25.1 4.2 %collective-permute-start = (bf16[80,512]{1,0:T(8,128)(2,1)}, bf16[80,512]{1,0:T(8,128)(2,1)S(1)}, u32[]{:S(2)}, u32[]{:S(2)}) collective-permute-start(bf16[80,512]{1,0:T(8,128)(2,1)} %get-tuple-element.1949), channel_id=1, source_target_pairs={{0,16},{1,17},{2,18},{3,19},{4,20},{5,21},{6,22},{7,23},{8,24},{9,... | collective-permute-start | bytes 245768 | tf_op jit(solution)/shard_map/while/body/eval_jaxpr/ppermute | solution.py:35
  29.3 2.3 collective-permute-done
  33.3 4.1 %collective-permute-start.4 = (bf16[1,80,1,128]{3,2,1,0:T(2,128)(2,1)}, bf16[1,80,1,128]{3,2,1,0:T(2,128)(2,1)}, u32[]{:S(2)}, u32[]{:S(2)}) collective-permute-start(bf16[1,80,1,128]{3,2,1,0:T(2,128)(2,1)} %slice.249), channel_id=1, source_target_pairs={{0,4},{4,8},{8,12},{1,5},{5,9},{9,13},{2,6},{6,10},{10,14},{3,7},{... | collective-permute-start | bytes 61448 | tf_op jit(solution)/shard_map/ppermute | solution.py:23
  77.6 39.4 %while.78 = (s32[]{:T(128)}, f32[1,320,1024]{2,1,0:T(8,128)}, bf16[80,512]{1,0:T(8,128)(2,1)}, bf16[80,1024]{1,0:T(8,128)(2,1)}, s32[]{:T(128)}, /*index=5*/f32[...) while((s32[]{:T(128)}, f32[1,320,1024]{2,1,0:T(8,128)}, ...), condition=%wide.region_7.8_spmd.clone, body=%wide.region_4.7_spmd.clone.sunk | while | flops 735807488 | bytes 26063432 | solution.py:199
  78.9 7.5 %collective-permute-done.1 = bf16[80,512]{1,0:T(8,128)(2,1)S(1)} collective-permute-done((bf16[80,512]{1,0:T(8,128)(2,1)}, bf16[80,512]{1,0:T(8,128)(2,1)S(1)}, u32[]{:S(2)}, u32[]{:S(2)}) %collective-permute-start.1) | collective-permute-done | bytes 81952 | tf_op jit(solution)/shard_map/while/body/eval_jaxpr/ppermute | solution.py:35
  88.3 8.3 %collective-permute-done.1 = bf16[80,512]{1,0:T(8,128)(2,1)S(1)} collective-permute-done((bf16[80,512]{1,0:T(8,128)(2,1)}, bf16[80,512]{1,0:T(8,128)(2,1)S(1)}, u32[]{:S(2)}, u32[]{:S(2)}) %collective-permute-start.1) | collective-permute-done | bytes 81952 | tf_op jit(solution)/shard_map/while/body/eval_jaxpr/ppermute | solution.py:35
  96.6 6.6 %conditional.13 = (f32[1,320,1024]{2,1,0:T(8,128)}, bf16[80,1024]{1,0:T(8,128)(2,1)}, bf16[80,512]{1,0:T(8,128)(2,1)}) conditional(s32[]{:T(128)} %convert_element_type.237, (f32[1,320,1024]{2,1,0:T(8,128)}, bf16[80,1024]{1,0:T(8,128)(2,1)}) %tuple.213, (s32[]{:T(128)}, s32[1024]{0:T(1024)S(1)}, f32[1,320,8,128]{3,2,1,0:T(8,128)S(1)}, ...), branch_computations={%region_5.5_spmd, %region_6.6_spmd} | conditional | flops 735807488 | bytes 25719022 | solution.py:189
  104.5 5.9 %collective-permute-done.1 = bf16[80,512]{1,0:T(8,128)(2,1)S(1)} collective-permute-done((bf16[80,512]{1,0:T(8,128)(2,1)}, bf16[80,512]{1,0:T(8,128)(2,1)S(1)}, u32[]{:S(2)}, u32[]{:S(2)}) %collective-permute-start.1) | collective-permute-done | bytes 81952 | tf_op jit(solution)/shard_map/while/body/eval_jaxpr/ppermute | solution.py:35
  110.4 6.6 %conditional.13 = (f32[1,320,1024]{2,1,0:T(8,128)}, bf16[80,1024]{1,0:T(8,128)(2,1)}, bf16[80,512]{1,0:T(8,128)(2,1)}) conditional(s32[]{:T(128)} %convert_element_type.237, (f32[1,320,1024]{2,1,0:T(8,128)}, bf16[80,1024]{1,0:T(8,128)(2,1)}) %tuple.213, (s32[]{:T(128)}, s32[1024]{0:T(1024)S(1)}, f32[1,320,8,128]{3,2,1,0:T(8,128)S(1)}, ...), branch_computations={%region_5.5_spmd, %region_6.6_spmd} | conditional | flops 735807488 | bytes 25719022 | solution.py:189
  120.2 3.0 %collective-permute-start.10 = (bf16[1,80,8,1]{3,2,1,0:T(8,128)(2,1)S(1)}, bf16[1,80,8,1]{3,2,1,0:T(8,128)(2,1)S(1)}, u32[]{:S(2)}, u32[]{:S(2)}) collective-permute-start(bf16[1,80,8,1]{3,2,1,0:T(8,128)(2,1)S(1)} %slice.269), channel_id=1, source_target_pairs={{0,1},{1,2},{2,3},{4,5},{5,6},{6,7},{8,9},{9,10},{10,11},{12,13},{... | collective-permute-start | bytes 3848 | tf_op jit(solution)/shard_map/ppermute | solution.py:23
  124.6 5.8 %collective-permute-start.8 = (bf16[1,80,1,128]{3,2,1,0:T(2,128)(2,1)S(1)}, bf16[1,80,1,128]{3,2,1,0:T(2,128)(2,1)}, u32[]{:S(2)}, u32[]{:S(2)}) collective-permute-start(bf16[1,80,1,128]{3,2,1,0:T(2,128)(2,1)S(1)} %slice.263), channel_id=1, source_target_pairs={{0,4},{4,8},{8,12},{1,5},{5,9},{9,13},{2,6},{6,10},{10,14},{3,7},{... | collective-permute-start | bytes 61448 | tf_op jit(solution)/shard_map/ppermute | solution.py:23
  150.4 28.3 %while.79 = (s32[]{:T(128)}, f32[1,320,1024]{2,1,0:T(8,128)}, bf16[80,512]{1,0:T(8,128)(2,1)}, bf16[80,1024]{1,0:T(8,128)(2,1)}, s32[]{:T(128)}, /*index=5*/f32[...) while((s32[]{:T(128)}, f32[1,320,1024]{2,1,0:T(8,128)}, ...), condition=%wide.region_11.12_spmd.clone, body=%wide.region_8.11_spmd.clone.sunk | while | flops 735807488 | bytes 26063432 | solution.py:199
  151.7 2.3 collective-permute-done.2
  154.1 6.6 %conditional.14 = (f32[1,320,1024]{2,1,0:T(8,128)}, bf16[80,1024]{1,0:T(8,128)(2,1)}, bf16[80,512]{1,0:T(8,128)(2,1)}) conditional(s32[]{:T(128)} %convert_element_type.238, (f32[1,320,1024]{2,1,0:T(8,128)}, bf16[80,1024]{1,0:T(8,128)(2,1)}) %tuple.216, (s32[]{:T(128)}, s32[1024]{0:T(1024)S(1)}, f32[1,320,8,128]{3,2,1,0:T(8,128)S(1)}, ...), branch_computations={%region_9.9_spmd, %region_10.10_spmd} | conditional | flops 735807488 | bytes 25719022 | solution.py:189
  164.3 6.6 %conditional.14 = (f32[1,320,1024]{2,1,0:T(8,128)}, bf16[80,1024]{1,0:T(8,128)(2,1)}, bf16[80,512]{1,0:T(8,128)(2,1)}) conditional(s32[]{:T(128)} %convert_element_type.238, (f32[1,320,1024]{2,1,0:T(8,128)}, bf16[80,1024]{1,0:T(8,128)(2,1)}) %tuple.216, (s32[]{:T(128)}, s32[1024]{0:T(1024)S(1)}, f32[1,320,8,128]{3,2,1,0:T(8,128)S(1)}, ...), branch_computations={%region_9.9_spmd, %region_10.10_spmd} | conditional | flops 735807488 | bytes 25719022 | solution.py:189
  170.8 4.2 %collective-permute-start.2 = (bf16[80,512]{1,0:T(8,128)(2,1)}, bf16[80,512]{1,0:T(8,128)(2,1)S(1)}, u32[]{:S(2)}, u32[]{:S(2)}) collective-permute-start(bf16[80,512]{1,0:T(8,128)(2,1)} %get-tuple-element.2039), channel_id=1, source_target_pairs={{0,16},{1,17},{2,18},{3,19},{4,20},{5,21},{6,22},{7,23},{8,24},{9,... | collective-permute-start | bytes 245768 | tf_op jit(solution)/shard_map/while/body/eval_jaxpr/ppermute | solution.py:35
  175.0 3.0 %collective-permute-done.2 = bf16[80,512]{1,0:T(8,128)(2,1)S(1)} collective-permute-done((bf16[80,512]{1,0:T(8,128)(2,1)}, bf16[80,512]{1,0:T(8,128)(2,1)S(1)}, u32[]{:S(2)}, u32[]{:S(2)}) %collective-permute-start.2) | collective-permute-done | bytes 81952 | tf_op jit(solution)/shard_map/while/body/eval_jaxpr/ppermute | solution.py:35
  181.8 3.0 %collective-permute-start.14 = (bf16[1,80,8,1]{3,2,1,0:T(8,128)(2,1)S(1)}, bf16[1,80,8,1]{3,2,1,0:T(8,128)(2,1)S(1)}, u32[]{:S(2)}, u32[]{:S(2)}) collective-permute-start(bf16[1,80,8,1]{3,2,1,0:T(8,128)(2,1)S(1)} %slice.281), channel_id=1, source_target_pairs={{0,1},{1,2},{2,3},{4,5},{5,6},{6,7},{8,9},{9,10},{10,11},{12,13},{... | collective-permute-start | bytes 3848 | tf_op jit(solution)/shard_map/ppermute | solution.py:23
  187.4 5.1 %collective-permute-start.12 = (bf16[1,80,1,128]{3,2,1,0:T(2,128)(2,1)}, bf16[1,80,1,128]{3,2,1,0:T(2,128)(2,1)}, u32[]{:S(2)}, u32[]{:S(2)}) collective-permute-start(bf16[1,80,1,128]{3,2,1,0:T(2,128)(2,1)} %slice.275), channel_id=1, source_target_pairs={{0,4},{4,8},{8,12},{1,5},{5,9},{9,13},{2,6},{6,10},{10,14},{3,7},{... | collective-permute-start | bytes 61448 | tf_op jit(solution)/shard_map/ppermute | solution.py:23
  203.9 38.9 %while.80 = (s32[]{:T(128)}, f32[1,320,1024]{2,1,0:T(8,128)}, bf16[80,512]{1,0:T(8,128)(2,1)}, s32[]{:T(128)}, f32[1,320,8,128]{3,2,1,0:T(8,128)S(1)}, /*index=5...) while((s32[]{:T(128)}, f32[1,320,1024]{2,1,0:T(8,128)}, ...), condition=%wide.region_15.16_spmd.clone, body=%wide.region_12.15_spmd.clone.sunk | while | flops 735807488 | bytes 24588772 | solution.py:199
  205.2 11.1 %collective-permute-done.3 = bf16[80,512]{1,0:T(8,128)(2,1)S(1)} collective-permute-done((bf16[80,512]{1,0:T(8,128)(2,1)}, bf16[80,512]{1,0:T(8,128)(2,1)S(1)}, u32[]{:S(2)}, u32[]{:S(2)}) %collective-permute-start.3) | collective-permute-done | bytes 81952 | tf_op jit(solution)/shard_map/while/body/eval_jaxpr/ppermute | solution.py:35
  218.2 7.6 %collective-permute-done.3 = bf16[80,512]{1,0:T(8,128)(2,1)S(1)} collective-permute-done((bf16[80,512]{1,0:T(8,128)(2,1)}, bf16[80,512]{1,0:T(8,128)(2,1)S(1)}, u32[]{:S(2)}, u32[]{:S(2)}) %collective-permute-start.3) | collective-permute-done | bytes 81952 | tf_op jit(solution)/shard_map/while/body/eval_jaxpr/ppermute | solution.py:35
  225.8 5.2 %conditional.15 = (f32[1,320,1024]{2,1,0:T(8,128)}, bf16[80,512]{1,0:T(8,128)(2,1)}) conditional(s32[]{:T(128)} %convert_element_type.239, f32[1,320,1024]{2,1,0:T(8,128)} %get-tuple-element.2085, (s32[]{:T(128)}, s32[1024]{0:T(1024)S(1)}, f32[1,320,8,128]{3,2,1,0:T(8,128)S(1)}, pred[1,5,2,1024]{3,2,1,0:T(4,128)(4,1)S(1)}, ...), branch_computations={%region_13.13_spmd, %region_14.14_spmd} | conditional | flops 735807488 | bytes 24244394 | solution.py:189
  232.3 5.3 %collective-permute-done.3 = bf16[80,512]{1,0:T(8,128)(2,1)S(1)} collective-permute-done((bf16[80,512]{1,0:T(8,128)(2,1)}, bf16[80,512]{1,0:T(8,128)(2,1)S(1)}, u32[]{:S(2)}, u32[]{:S(2)}) %collective-permute-start.3) | collective-permute-done | bytes 81952 | tf_op jit(solution)/shard_map/while/body/eval_jaxpr/ppermute | solution.py:35
  237.6 5.2 %conditional.15 = (f32[1,320,1024]{2,1,0:T(8,128)}, bf16[80,512]{1,0:T(8,128)(2,1)}) conditional(s32[]{:T(128)} %convert_element_type.239, f32[1,320,1024]{2,1,0:T(8,128)} %get-tuple-element.2085, (s32[]{:T(128)}, s32[1024]{0:T(1024)S(1)}, f32[1,320,8,128]{3,2,1,0:T(8,128)S(1)}, pred[1,5,2,1024]{3,2,1,0:T(4,128)(4,1)S(1)}, ...), branch_computations={%region_13.13_spmd, %region_14.14_spmd} | conditional | flops 735807488 | bytes 24244394 | solution.py:189
  242.8 2.6 %copy.34 = f32[40,8,8,128]{3,2,1,0:T(8,128)} copy(f32[40,8,8,128]{3,1,2,0:T(8,128)} %bitcast.259) | data formatting | bytes 2621440
  (335 shorter events, 151.6 us)
Async XLA Ops:
  7.4 7.2 %collective-permute-start = (bf16[80,512]{1,0:T(8,128)(2,1)}, bf16[80,512]{1,0:T(8,128)(2,1)S(1)}, u32[]{:S(2)}, u32[]{:S(2)}) collective-permute-start(bf16[80,512]{1,0:T(8,128)(2,1)} %get-tuple-element.1949), channel_id=1, source_target_pairs={{0,16},{1,17},{2,18},{3,19},{4,20},{5,21},{6,22},{7,23},{8,24},{9,... | collective-permute-start | bytes 245768 | tf_op jit(solution)/shard_map/while/body/eval_jaxpr/ppermute | solution.py:35
  17.9 3.9 %collective-permute-start = (bf16[80,512]{1,0:T(8,128)(2,1)}, bf16[80,512]{1,0:T(8,128)(2,1)S(1)}, u32[]{:S(2)}, u32[]{:S(2)}) collective-permute-start(bf16[80,512]{1,0:T(8,128)(2,1)} %get-tuple-element.1949), channel_id=1, source_target_pairs={{0,16},{1,17},{2,18},{3,19},{4,20},{5,21},{6,22},{7,23},{8,24},{9,... | collective-permute-start | bytes 245768 | tf_op jit(solution)/shard_map/while/body/eval_jaxpr/ppermute | solution.py:35
  25.1 6.5 %collective-permute-start = (bf16[80,512]{1,0:T(8,128)(2,1)}, bf16[80,512]{1,0:T(8,128)(2,1)S(1)}, u32[]{:S(2)}, u32[]{:S(2)}) collective-permute-start(bf16[80,512]{1,0:T(8,128)(2,1)} %get-tuple-element.1949), channel_id=1, source_target_pairs={{0,16},{1,17},{2,18},{3,19},{4,20},{5,21},{6,22},{7,23},{8,24},{9,... | collective-permute-start | bytes 245768 | tf_op jit(solution)/shard_map/while/body/eval_jaxpr/ppermute | solution.py:35
  32.3 14.5 %copy-start.1 = (f32[1,320,1024]{2,1,0:T(8,128)}, f32[1,320,1024]{2,1,0:T(8,128)S(1)}, u32[]{:S(2)}) copy-start(f32[1,320,1024]{2,1,0:T(8,128)S(1)} %get-tuple-element.1974) | copy-start | bytes 3932164
  32.5 11.7 %copy-start.13 = (bf16[2,6,80,320]{3,2,1,0:T(8,128)(2,1)S(1)}, bf16[2,6,80,320]{3,2,1,0:T(8,128)(2,1)}, u32[]{:S(2)}) copy-start(bf16[2,6,80,320]{3,2,1,0:T(8,128)(2,1)} %param.23) | copy-start | bytes 1843204
  33.3 29.9 %collective-permute-start.4 = (bf16[1,80,1,128]{3,2,1,0:T(2,128)(2,1)}, bf16[1,80,1,128]{3,2,1,0:T(2,128)(2,1)}, u32[]{:S(2)}, u32[]{:S(2)}) collective-permute-start(bf16[1,80,1,128]{3,2,1,0:T(2,128)(2,1)} %slice.249), channel_id=1, source_target_pairs={{0,4},{4,8},{8,12},{1,5},{5,9},{9,13},{2,6},{6,10},{10,14},{3,7},{... | collective-permute-start | bytes 61448 | tf_op jit(solution)/shard_map/ppermute | solution.py:23
  37.4 29.1 %collective-permute-start.5 = (bf16[1,80,1,128]{3,2,1,0:T(2,128)(2,1)S(1)}, bf16[1,80,1,128]{3,2,1,0:T(2,128)(2,1)}, u32[]{:S(2)}, u32[]{:S(2)}) collective-permute-start(bf16[1,80,1,128]{3,2,1,0:T(2,128)(2,1)S(1)} %slice.253), channel_id=1, source_target_pairs={{4,0},{8,4},{12,8},{5,1},{9,5},{13,9},{6,2},{10,6},{14,10},{7,3},{... | collective-permute-start | bytes 61448 | tf_op jit(solution)/shard_map/ppermute | solution.py:25
  40.9 15.4 %collective-permute-start.6 = (bf16[1,80,8,1]{3,2,1,0:T(8,128)(2,1)}, bf16[1,80,8,1]{3,2,1,0:T(8,128)(2,1)}, u32[]{:S(2)}, u32[]{:S(2)}) collective-permute-start(bf16[1,80,8,1]{3,2,1,0:T(8,128)(2,1)} %slice.255), channel_id=1, source_target_pairs={{0,1},{1,2},{2,3},{4,5},{5,6},{6,7},{8,9},{9,10},{10,11},{12,13},{... | collective-permute-start | bytes 3848 | tf_op jit(solution)/shard_map/ppermute | solution.py:23
  42.9 15.1 %collective-permute-start.7 = (bf16[1,80,8,1]{3,2,1,0:T(8,128)(2,1)}, bf16[1,80,8,1]{3,2,1,0:T(8,128)(2,1)}, u32[]{:S(2)}, u32[]{:S(2)}) collective-permute-start(bf16[1,80,8,1]{3,2,1,0:T(8,128)(2,1)} %bitcast.237), channel_id=1, source_target_pairs={{1,0},{2,1},{3,2},{5,4},{6,5},{7,6},{9,8},{10,9},{11,10},{13,12},{... | collective-permute-start | bytes 3848 | tf_op jit(solution)/shard_map/ppermute | solution.py:25
  77.6 8.8 %collective-permute-start.1 = (bf16[80,512]{1,0:T(8,128)(2,1)}, bf16[80,512]{1,0:T(8,128)(2,1)S(1)}, u32[]{:S(2)}, u32[]{:S(2)}) collective-permute-start(bf16[80,512]{1,0:T(8,128)(2,1)} %get-tuple-element.1991), channel_id=1, source_target_pairs={{16,0},{17,1},{18,2},{19,3},{20,4},{21,5},{22,6},{23,7},{24,8},{25... | collective-permute-start | bytes 245768 | tf_op jit(solution)/shard_map/while/body/eval_jaxpr/ppermute | solution.py:35
  87.0 9.6 %collective-permute-start.1 = (bf16[80,512]{1,0:T(8,128)(2,1)}, bf16[80,512]{1,0:T(8,128)(2,1)S(1)}, u32[]{:S(2)}, u32[]{:S(2)}) collective-permute-start(bf16[80,512]{1,0:T(8,128)(2,1)} %get-tuple-element.1991), channel_id=1, source_target_pairs={{16,0},{17,1},{18,2},{19,3},{20,4},{21,5},{22,6},{23,7},{24,8},{25... | collective-permute-start | bytes 245768 | tf_op jit(solution)/shard_map/while/body/eval_jaxpr/ppermute | solution.py:35
  103.2 7.2 %collective-permute-start.1 = (bf16[80,512]{1,0:T(8,128)(2,1)}, bf16[80,512]{1,0:T(8,128)(2,1)S(1)}, u32[]{:S(2)}, u32[]{:S(2)}) collective-permute-start(bf16[80,512]{1,0:T(8,128)(2,1)} %get-tuple-element.1991), channel_id=1, source_target_pairs={{16,0},{17,1},{18,2},{19,3},{20,4},{21,5},{22,6},{23,7},{24,8},{25... | collective-permute-start | bytes 245768 | tf_op jit(solution)/shard_map/while/body/eval_jaxpr/ppermute | solution.py:35
  118.5 11.9 %copy-start.25 = (bf16[80,1024]{1,0:T(8,128)(2,1)S(1)}, bf16[80,1024]{1,0:T(8,128)(2,1)}, u32[]{:S(2)}) copy-start(bf16[80,1024]{1,0:T(8,128)(2,1)} %get-tuple-element.1287) | copy-start | bytes 491524
  118.7 5.8 %copy-start.18 = (bf16[1,5,4,1,4,8,128]{6,5,4,3,2,1,0:T(8,128)(2,1)}, bf16[1,5,4,1,4,8,128]{6,5,4,3,2,1,0:T(8,128)(2,1)S(1)}, u32[]{:S(2)}) copy-start(bf16[1,5,4,1,4,8,128]{6,5,4,3,2,1,0:T(8,128)(2,1)S(1)} %get-tuple-element.1583) | copy-start | bytes 491524
  118.7 12.5 %collective-permute-start.11 = (bf16[1,80,8,1]{3,2,1,0:T(8,128)(2,1)S(1)}, bf16[1,80,8,1]{3,2,1,0:T(8,128)(2,1)S(1)}, u32[]{:S(2)}, u32[]{:S(2)}) collective-permute-start(bf16[1,80,8,1]{3,2,1,0:T(8,128)(2,1)S(1)} %bitcast.296), channel_id=1, source_target_pairs={{1,0},{2,1},{3,2},{5,4},{6,5},{7,6},{9,8},{10,9},{11,10},{13,12},{... | collective-permute-start | bytes 3848 | tf_op jit(solution)/shard_map/ppermute | solution.py:25
  120.2 11.9 %collective-permute-start.10 = (bf16[1,80,8,1]{3,2,1,0:T(8,128)(2,1)S(1)}, bf16[1,80,8,1]{3,2,1,0:T(8,128)(2,1)S(1)}, u32[]{:S(2)}, u32[]{:S(2)}) collective-permute-start(bf16[1,80,8,1]{3,2,1,0:T(8,128)(2,1)S(1)} %slice.269), channel_id=1, source_target_pairs={{0,1},{1,2},{2,3},{4,5},{5,6},{6,7},{8,9},{9,10},{10,11},{12,13},{... | collective-permute-start | bytes 3848 | tf_op jit(solution)/shard_map/ppermute | solution.py:23
  123.2 12.9 %collective-permute-start.9 = (bf16[1,80,1,128]{3,2,1,0:T(2,128)(2,1)S(1)}, bf16[1,80,1,128]{3,2,1,0:T(2,128)(2,1)}, u32[]{:S(2)}, u32[]{:S(2)}) collective-permute-start(bf16[1,80,1,128]{3,2,1,0:T(2,128)(2,1)S(1)} %slice.267), channel_id=1, source_target_pairs={{4,0},{8,4},{12,8},{5,1},{9,5},{13,9},{6,2},{10,6},{14,10},{7,3},{... | collective-permute-start | bytes 61448 | tf_op jit(solution)/shard_map/ppermute | solution.py:25
  124.6 14.8 %collective-permute-start.8 = (bf16[1,80,1,128]{3,2,1,0:T(2,128)(2,1)S(1)}, bf16[1,80,1,128]{3,2,1,0:T(2,128)(2,1)}, u32[]{:S(2)}, u32[]{:S(2)}) collective-permute-start(bf16[1,80,1,128]{3,2,1,0:T(2,128)(2,1)S(1)} %slice.263), channel_id=1, source_target_pairs={{0,4},{4,8},{8,12},{1,5},{5,9},{9,13},{2,6},{6,10},{10,14},{3,7},{... | collective-permute-start | bytes 61448 | tf_op jit(solution)/shard_map/ppermute | solution.py:23
  137.7 12.7 %copy-start.9 = (bf16[320,160]{1,0:T(8,128)(2,1)S(1)}, bf16[320,160]{1,0:T(8,128)(2,1)}, u32[]{:S(2)}) copy-start(bf16[320,160]{1,0:T(8,128)(2,1)} %get-tuple-element.2121) | copy-start | bytes 307204
  150.4 3.6 %collective-permute-start.2 = (bf16[80,512]{1,0:T(8,128)(2,1)}, bf16[80,512]{1,0:T(8,128)(2,1)S(1)}, u32[]{:S(2)}, u32[]{:S(2)}) collective-permute-start(bf16[80,512]{1,0:T(8,128)(2,1)} %get-tuple-element.2039), channel_id=1, source_target_pairs={{0,16},{1,17},{2,18},{3,19},{4,20},{5,21},{6,22},{7,23},{8,24},{9,... | collective-permute-start | bytes 245768 | tf_op jit(solution)/shard_map/while/body/eval_jaxpr/ppermute | solution.py:35
  160.6 3.6 %collective-permute-start.2 = (bf16[80,512]{1,0:T(8,128)(2,1)}, bf16[80,512]{1,0:T(8,128)(2,1)S(1)}, u32[]{:S(2)}, u32[]{:S(2)}) collective-permute-start(bf16[80,512]{1,0:T(8,128)(2,1)} %get-tuple-element.2039), channel_id=1, source_target_pairs={{0,16},{1,17},{2,18},{3,19},{4,20},{5,21},{6,22},{7,23},{8,24},{9,... | collective-permute-start | bytes 245768 | tf_op jit(solution)/shard_map/while/body/eval_jaxpr/ppermute | solution.py:35
  170.8 7.2 %collective-permute-start.2 = (bf16[80,512]{1,0:T(8,128)(2,1)}, bf16[80,512]{1,0:T(8,128)(2,1)S(1)}, u32[]{:S(2)}, u32[]{:S(2)}) collective-permute-start(bf16[80,512]{1,0:T(8,128)(2,1)} %get-tuple-element.2039), channel_id=1, source_target_pairs={{0,16},{1,17},{2,18},{3,19},{4,20},{5,21},{6,22},{7,23},{8,24},{9,... | collective-permute-start | bytes 245768 | tf_op jit(solution)/shard_map/while/body/eval_jaxpr/ppermute | solution.py:35
  180.2 12.4 %copy-start.28 = (bf16[80,1024]{1,0:T(8,128)(2,1)S(1)}, bf16[80,1024]{1,0:T(8,128)(2,1)}, u32[]{:S(2)}) copy-start(bf16[80,1024]{1,0:T(8,128)(2,1)} %get-tuple-element.1289) | copy-start | bytes 491524
  180.4 13.0 %collective-permute-start.15 = (bf16[1,80,8,1]{3,2,1,0:T(8,128)(2,1)S(1)}, bf16[1,80,8,1]{3,2,1,0:T(8,128)(2,1)S(1)}, u32[]{:S(2)}, u32[]{:S(2)}) collective-permute-start(bf16[1,80,8,1]{3,2,1,0:T(8,128)(2,1)S(1)} %bitcast.298), channel_id=1, source_target_pairs={{1,0},{2,1},{3,2},{5,4},{6,5},{7,6},{9,8},{10,9},{11,10},{13,12},{... | collective-permute-start | bytes 3848 | tf_op jit(solution)/shard_map/ppermute | solution.py:25
  181.8 11.8 %collective-permute-start.14 = (bf16[1,80,8,1]{3,2,1,0:T(8,128)(2,1)S(1)}, bf16[1,80,8,1]{3,2,1,0:T(8,128)(2,1)S(1)}, u32[]{:S(2)}, u32[]{:S(2)}) collective-permute-start(bf16[1,80,8,1]{3,2,1,0:T(8,128)(2,1)S(1)} %slice.281), channel_id=1, source_target_pairs={{0,1},{1,2},{2,3},{4,5},{5,6},{6,7},{8,9},{9,10},{10,11},{12,13},{... | collective-permute-start | bytes 3848 | tf_op jit(solution)/shard_map/ppermute | solution.py:23
  185.5 10.0 %collective-permute-start.13 = (bf16[1,80,1,128]{3,2,1,0:T(2,128)(2,1)}, bf16[1,80,1,128]{3,2,1,0:T(2,128)(2,1)}, u32[]{:S(2)}, u32[]{:S(2)}) collective-permute-start(bf16[1,80,1,128]{3,2,1,0:T(2,128)(2,1)} %slice.279), channel_id=1, source_target_pairs={{4,0},{8,4},{12,8},{5,1},{9,5},{13,9},{6,2},{10,6},{14,10},{7,3},{... | collective-permute-start | bytes 61448 | tf_op jit(solution)/shard_map/ppermute | solution.py:25
  187.4 10.6 %collective-permute-start.12 = (bf16[1,80,1,128]{3,2,1,0:T(2,128)(2,1)}, bf16[1,80,1,128]{3,2,1,0:T(2,128)(2,1)}, u32[]{:S(2)}, u32[]{:S(2)}) collective-permute-start(bf16[1,80,1,128]{3,2,1,0:T(2,128)(2,1)} %slice.275), channel_id=1, source_target_pairs={{0,4},{4,8},{8,12},{1,5},{5,9},{9,13},{2,6},{6,10},{10,14},{3,7},{... | collective-permute-start | bytes 61448 | tf_op jit(solution)/shard_map/ppermute | solution.py:23
  195.4 8.5 %copy-start.11 = (bf16[320,160]{1,0:T(8,128)(2,1)S(1)}, bf16[320,160]{1,0:T(8,128)(2,1)}, u32[]{:S(2)}) copy-start(bf16[320,160]{1,0:T(8,128)(2,1)} %copy-done.10) | copy-start | bytes 307204
  195.4 8.5 %copy-start.19 = (pred[1,5,2,1024]{3,2,1,0:T(4,128)(4,1)S(1)}, pred[1,5,2,1024]{3,2,1,0:T(4,128)(4,1)}, u32[]{:S(2)}) copy-start(pred[1,5,2,1024]{3,2,1,0:T(4,128)(4,1)} %get-tuple-element.2127) | copy-start | bytes 30724
  203.9 12.4 %collective-permute-start.3 = (bf16[80,512]{1,0:T(8,128)(2,1)}, bf16[80,512]{1,0:T(8,128)(2,1)S(1)}, u32[]{:S(2)}, u32[]{:S(2)}) collective-permute-start(bf16[80,512]{1,0:T(8,128)(2,1)} %get-tuple-element.2086), channel_id=1, source_target_pairs={{16,0},{17,1},{18,2},{19,3},{20,4},{21,5},{22,6},{23,7},{24,8},{25... | collective-permute-start | bytes 245768 | tf_op jit(solution)/shard_map/while/body/eval_jaxpr/ppermute | solution.py:35
  216.9 8.9 %collective-permute-start.3 = (bf16[80,512]{1,0:T(8,128)(2,1)}, bf16[80,512]{1,0:T(8,128)(2,1)S(1)}, u32[]{:S(2)}, u32[]{:S(2)}) collective-permute-start(bf16[80,512]{1,0:T(8,128)(2,1)} %get-tuple-element.2086), channel_id=1, source_target_pairs={{16,0},{17,1},{18,2},{19,3},{20,4},{21,5},{22,6},{23,7},{24,8},{25... | collective-permute-start | bytes 245768 | tf_op jit(solution)/shard_map/while/body/eval_jaxpr/ppermute | solution.py:35
  231.0 6.6 %collective-permute-start.3 = (bf16[80,512]{1,0:T(8,128)(2,1)}, bf16[80,512]{1,0:T(8,128)(2,1)S(1)}, u32[]{:S(2)}, u32[]{:S(2)}) collective-permute-start(bf16[80,512]{1,0:T(8,128)(2,1)} %get-tuple-element.2086), channel_id=1, source_target_pairs={{16,0},{17,1},{18,2},{19,3},{20,4},{21,5},{22,6},{23,7},{24,8},{25... | collective-permute-start | bytes 245768 | tf_op jit(solution)/shard_map/while/body/eval_jaxpr/ppermute | solution.py:35
  (39 other events, 66.5 us)
where the time goes:
time: 248 us; the launch traced here: 245 us
  local copies, waits for them, and re-layouts  96.5 us (39%)
  waiting for transfers between devices  60.4 us (24%)
  starting transfers between devices  55.8 us (22%)
  other arithmetic  21.8 us (9%)
  matrix products  9.5 us (4%)
    ppermute x12, waiting for transfers between devices, passed_along(): lax.ppermute(value, axis, [(source, source + steps) for source in range(i...  60.4 us
    ppermute x12, starting transfers between devices, passed_along(): lax.ppermute(value, axis, [(source, source + steps) for source in range(i...  24.9 us
    ppermute x6, starting transfers between devices, extended(): lax.ppermute(tail, axis, [(i, (i + 1) % count) for i in range(ends)])  23.2 us
    unnamed x59, local copies, waits for them, and re-layouts  22.5 us
    another operation x15, local copies, waits for them, and re-layouts, run_half(): jnp.stack([other_side, from_xlow, from_xhigh, from_ylow, from_yhigh], axi...  20.2 us
    cond x60, local copies, waits for them, and re-layouts  16.5 us
    broadcast_in_dim x20, local copies, waits for them, and re-layouts, coupling_product(): jnp.where(face_mask[:, :, None, :], incoming[:, None], jnp.zeros((), jnp....  9.16 us
    ppermute x6, starting transfers between devices, extended(): lax.ppermute(head, axis, [((i + 1) % count, i) for i in range(ends)])  7.73 us
  transfers between devices with their start and end apart: 24, of which 12 were waited for; matrix products, arithmetic and copies ran while one was open for 16% of the time, Pallas kernels for 0%

commit v1 on v0

v1 whole, which is shorter than its diff:
```python
import functools
import jax
import jax.numpy as jnp
from jax import lax
from jax.experimental import pallas as pl
from jax.experimental.pallas import tpu as pltpu
from jax.sharding import PartitionSpec as P

NVAR = 5
NP = 4
BLOCK = 320
TRACE = 80
KD = 4
KC = 2
SWEEPS = 2
HALVES = 2 * SWEEPS
LANES = 128
GROUP = 4
MESH = pl.DeviceIdType.MESH
F32 = jnp.float32
BF16 = jnp.bfloat16


def kernel(
    rows,
    rhs_ref,
    inv_ref,
    lat_ref,
    chain_ref,
    kind_ref,
    face_ref,
    out_ref,
    u_ref,
    base_ref,
    prod_ref,
    tr_ref,
    lat_stack,
    chain_stack,
    inv_stack,
    front_in,
    front_out,
    x_in,
    x_out,
    y_in,
    y_out,
    front_send,
    front_recv,
    x_send,
    x_recv,
    y_send,
    y_recv,
):
    groups = rows // GROUP
    places = {}
    for name in ("sweep", "cx", "cy"):
        places[name] = (lax.axis_index(name), lax.axis_size(name))

    def has(name, step):
        spot, count = places[name]
        return spot < count - 1 if step > 0 else spot > 0

    def partner(name, step):
        return {name: places[name][0] + step}

    front_in[...] = jnp.zeros(front_in.shape, BF16)
    x_in[...] = jnp.zeros(x_in.shape, BF16)
    y_in[...] = jnp.zeros(y_in.shape, BF16)
    barrier = pltpu.get_barrier_semaphore()
    total = 0
    for name in ("sweep", "cx", "cy"):
        for step in (-1, 1):
            exists = has(name, step)
            total = total + jnp.where(exists, 1, 0)

            @pl.when(exists)
            def _():
                pl.semaphore_signal(
                    barrier, inc=1, device_id=partner(name, step), device_id_type=MESH
                )

    pl.semaphore_wait(barrier, total)

    lane = lax.broadcasted_iota(jnp.int32, (TRACE, LANES), 1)

    def front_copy(half, group, step):
        return pltpu.make_async_remote_copy(
            src_ref=front_out.at[half, group],
            dst_ref=front_in.at[half, group],
            send_sem=front_send.at[half, group],
            recv_sem=front_recv.at[half, group],
            device_id=partner("sweep", step),
            device_id_type=MESH,
        )

    def x_copy(half, side):
        return pltpu.make_async_remote_copy(
            src_ref=x_out.at[half, side],
            dst_ref=x_in.at[half, 1 - side],
            send_sem=x_send.at[half, side],
            recv_sem=x_recv.at[half, 1 - side],
            device_id=partner("cx", 2 * side - 1),
            device_id_type=MESH,
        )

    def y_copy(half, side):
        return pltpu.make_async_remote_copy(
            src_ref=y_out.at[half, side],
            dst_ref=y_in.at[half, 1 - side],
            send_sem=y_send.at[half, side],
            recv_sem=y_recv.at[half, 1 - side],
            device_id=partner("cy", 2 * side - 1),
            device_id_type=MESH,
        )

    def rhs_row(row):
        return rhs_ref[pl.ds(row, BLOCK, stride=rows), :]

    def put_masked(stack, place, lanes, value, face, row):
        one = face_ref[face, row : row + 1, :].astype(F32)
        stack[pl.ds(place, TRACE), lanes] = value * (1.0 - one).astype(BF16)
        stack[pl.ds(place + TRACE, TRACE), lanes] = value * one.astype(BF16)

    def edge_x(row, side):
        first = (NP - 1) * NP * side
        for node in range(NP):
            tr_ref[pl.ds(node, NVAR * NP, stride=NP), :] = u_ref[
                row, pl.ds(first + node, NVAR * NP, stride=NP * NP), :
            ]
        return tr_ref[...]

    def edge_y(row, side):
        return u_ref[row, pl.ds((NP - 1) * side, TRACE, stride=NP), :]

    def lateral(half, group):
        for local in range(GROUP):
            row = group * GROUP + local
            lanes = slice(local * LANES, (local + 1) * LANES)
            if row > 0:
                from_xlow = edge_x(row - 1, 1).astype(BF16)
            else:
                from_xlow = x_in[half, 0]
            put_masked(lat_stack, 0, lanes, from_xlow, 2, row)
            if row < rows - 1:
                from_xhigh = edge_x(row + 1, 0).astype(BF16)
            else:
                from_xhigh = x_in[half, 1]
            put_masked(lat_stack, 2 * TRACE, lanes, from_xhigh, 3, row)
            seen = pltpu.roll(y_in[half, 0].astype(F32), (LANES - row) % LANES, 1)
            own = pltpu.roll(edge_y(row, 1), 1, 1)
            put_masked(
                lat_stack, 4 * TRACE, lanes, jnp.where(lane == 0, seen, own).astype(BF16), 4, row
            )
            seen = pltpu.roll(y_in[half, 1].astype(F32), LANES - 1 - row, 1)
            own = pltpu.roll(edge_y(row, 0), LANES - 1, 1)
            put_masked(
                lat_stack,
                6 * TRACE,
                lanes,
                jnp.where(lane == LANES - 1, seen, own).astype(BF16),
                5,
                row,
            )
        product = jnp.dot(lat_ref[...], lat_stack[...], preferred_element_type=F32)
        for local in range(GROUP):
            row = group * GROUP + local
            base_ref[row] = (
                rhs_row(row)
                - product[:, local * LANES : (local + 1) * LANES]
                - prod_ref[row]
            )

    for half in range(HALVES):
        forward = half % 2 == 0
        step = 1 if forward else -1
        upstream = has("sweep", -step)
        downstream = has("sweep", step)
        if half > 0:
            for side in range(2):

                @pl.when(has("cx", 2 * side - 1))
                def _():
                    x_copy(half - 1, 1 - side).wait_recv()

                @pl.when(has("cy", 2 * side - 1))
                def _():
                    y_copy(half - 1, 1 - side).wait_recv()

            for group in range(groups):
                lateral(half - 1, group)
        for group in range(groups):

            @pl.when(upstream)
            def _():
                front_copy(half, group, step).wait_recv()

            for local in range(GROUP):
                row = group * GROUP + local
                lanes = slice(local * LANES, (local + 1) * LANES)
                put_masked(
                    chain_stack, 0, lanes, front_in[half, group, local], 0 if forward else 1, row
                )
            product = jnp.dot(
                chain_ref[0 if forward else 1], chain_stack[...], preferred_element_type=F32
            )
            for local in range(GROUP):
                row = group * GROUP + local
                lanes = slice(local * LANES, (local + 1) * LANES)
                part = product[:, lanes]
                prod_ref[row] = part
                before = rhs_row(row) if half == 0 else base_ref[row]
                residual = (before - part).astype(BF16)
                kinds = kind_ref[row : row + 1, :]
                for kind in range(KD):
                    mask = jnp.where(kinds == kind, 1.0, 0.0).astype(BF16)
                    inv_stack[kind * BLOCK : (kind + 1) * BLOCK, lanes] = residual * mask
            updated = jnp.dot(inv_ref[...], inv_stack[...], preferred_element_type=F32)
            for local in range(GROUP):
                row = group * GROUP + local
                value = updated[:, local * LANES : (local + 1) * LANES]
                if half == HALVES - 1:
                    out_ref[pl.ds(row, BLOCK, stride=rows), :] = value
                else:
                    u_ref[row] = value
                first = NP * NP * (NP - 1) if forward else 0
                for var in range(NVAR):
                    start = var * NP * NP * NP + first
                    front_out[half, group, local, var * NP * NP : (var + 1) * NP * NP, :] = value[
                        start : start + NP * NP, :
                    ].astype(BF16)

            @pl.when(downstream)
            def _():
                front_copy(half, group, step).start()

        if half < HALVES - 1:
            for side in range(2):
                packed = jnp.zeros((TRACE, LANES), F32)
                for row in range(rows):
                    turned = pltpu.roll(edge_y(row, side), (row + side) % LANES, 1)
                    packed = jnp.where(lane == row, turned, packed)
                y_out[half, side] = packed.astype(BF16)

                @pl.when(has("cy", 2 * side - 1))
                def _():
                    y_copy(half, side).start()

                x_out[half, side] = edge_x((rows - 1) * side, side).astype(BF16)

                @pl.when(has("cx", 2 * side - 1))
                def _():
                    x_copy(half, side).start()

    for half in range(HALVES):
        step = 1 if half % 2 == 0 else -1

        @pl.when(has("sweep", step))
        def _():
            for group in range(groups):
                front_copy(half, group, step).wait_send()

        if half < HALVES - 1:
            for side in range(2):

                @pl.when(has("cy", 2 * side - 1))
                def _():
                    y_copy(half, side).wait_send()

                @pl.when(has("cx", 2 * side - 1))
                def _():
                    x_copy(half, side).wait_send()


def shards(right_side, inverse_table, coupling_table, block_kind, face_kind):
    _, _, rows, width_y = right_side.shape
    groups = rows // GROUP
    columns = GROUP * LANES
    inverse_wide = jnp.transpose(inverse_table, (1, 0, 2)).reshape(BLOCK, KD * BLOCK)
    coupling_wide = jnp.transpose(coupling_table, (3, 1, 0, 2))
    chain_wide = jnp.transpose(coupling_table[:, :2], (1, 3, 0, 2)).reshape(2, BLOCK, KC * TRACE)
    lateral_wide = coupling_wide[:, 2:].reshape(BLOCK, 4 * KC * TRACE)
    vmem = pl.BlockSpec(memory_space=pltpu.VMEM)
    result = pl.pallas_call(
        functools.partial(kernel, rows),
        out_shape=jax.ShapeDtypeStruct((BLOCK * rows, LANES), F32),
        in_specs=[vmem] * 6,
        out_specs=vmem,
        scratch_shapes=[
            pltpu.VMEM((rows, BLOCK, LANES), F32),
            pltpu.VMEM((rows, BLOCK, LANES), F32),
            pltpu.VMEM((rows, BLOCK, LANES), F32),
            pltpu.VMEM((TRACE, LANES), F32),
            pltpu.VMEM((4 * KC * TRACE, columns), BF16),
            pltpu.VMEM((KC * TRACE, columns), BF16),
            pltpu.VMEM((KD * BLOCK, columns), BF16),
            pltpu.VMEM((HALVES, groups, GROUP, TRACE, LANES), BF16),
            pltpu.VMEM((HALVES, groups, GROUP, TRACE, LANES), BF16),
            pltpu.VMEM((HALVES - 1, 2, TRACE, LANES), BF16),
            pltpu.VMEM((HALVES - 1, 2, TRACE, LANES), BF16),
            pltpu.VMEM((HALVES - 1, 2, TRACE, LANES), BF16),
            pltpu.VMEM((HALVES - 1, 2, TRACE, LANES), BF16),
            pltpu.SemaphoreType.DMA((HALVES, groups)),
            pltpu.SemaphoreType.DMA((HALVES, groups)),
            pltpu.SemaphoreType.DMA((HALVES - 1, 2)),
            pltpu.SemaphoreType.DMA((HALVES - 1, 2)),
            pltpu.SemaphoreType.DMA((HALVES - 1, 2)),
            pltpu.SemaphoreType.DMA((HALVES - 1, 2)),
        ],
        compiler_params=pltpu.CompilerParams(
            collective_id=0, has_side_effects=True, vmem_limit_bytes=48 << 20
        ),
    )(
        right_side.reshape(BLOCK * rows, width_y),
        inverse_wide,
        lateral_wide,
        chain_wide,
        block_kind.reshape(rows, width_y),
        face_kind.reshape(6, rows, width_y),
    )
    return result.reshape(right_side.shape)


def solution(mesh):
    in_specs = (
        P("sweep", None, "cx", "cy"),
        P(),
        P(),
        P("sweep", "cx", "cy"),
        P("sweep", None, "cx", "cy"),
    )
    out_specs = P("sweep", None, "cx", "cy")
    return jax.shard_map(shards, mesh=mesh, in_specs=in_specs, out_specs=out_specs, check_vma=False)
```

time: 248 us -> 52.1 us (0.21)
  local copies, waits for them, and re-layouts: 96.5 us -> 7.35 us
  waiting for transfers between devices: 60.4 us -> 0 us
  starting transfers between devices: 55.8 us -> 0 us
  Pallas kernels: 0 us -> 44.5 us
  other arithmetic: 21.8 us -> 0 us
  matrix products: 9.5 us -> 0 us
    ppermute x24 -> x0, waiting for transfers between devices: 60.4 us -> none  [the longest x12 60.4 us: passed_along(): lax.ppermute(value, axis, [(source, source + steps) for source in range(i...]
    ppermute x24 -> x0, starting transfers between devices: 55.8 us -> none  [the longest x12 24.9 us: passed_along(): lax.ppermute(value, axis, [(source, source + steps) for source in range(i...]
    pallas_call x0 -> x1, Pallas kernels: none -> 44.5 us  [shards(): pl.pallas_call(functools.partial(kernel, rows), out_shape=jax.ShapeDtypeS...]
    another operation x26 -> x0, local copies, waits for them, and re-layouts: 27.3 us -> none  [the longest x15 20.2 us: run_half(): jnp.stack([other_side, from_xlow, from_xhigh, from_ylow, from_yhigh], axi...]
    unnamed x59 -> x12, local copies, waits for them, and re-layouts: 22.5 us -> 1.94 us
    cond x60 -> x0, local copies, waits for them, and re-layouts: 16.5 us -> none
    concatenate x12 -> x0, other arithmetic: 15.7 us -> none  [the longest x3 4.88 us: start_traces(): jnp.concatenate([padded_x[:, :, 0:1], high_x[:, :, :-1]], axis=2)]
    slice x36 -> x3, local copies, waits for them, and re-layouts: 13.4 us -> 1.14 us  [the longest x1 1.04 us: shards(): coupling_table[:, :2]]
  transfers between devices with their start and end apart: 24 -> 0, of which waited for: 12 -> 0; matrix products, arithmetic and copies ran while one was open for 16% -> 0% of each run, Pallas kernels for 0% -> 0%
where the time goes in v1:
time: 52.1 us; the launch traced here: 51.9 us
  Pallas kernels  44.5 us (85%)
  local copies, waits for them, and re-layouts  7.35 us (14%)
    pallas_call x1, Pallas kernels, shards(): pl.pallas_call(functools.partial(kernel, rows), out_shape=jax.ShapeDtypeS...  44.5 us
    reshape x1, local copies, waits for them, and re-layouts, shards(): jnp.transpose(inverse_table, (1, 0, 2)).reshape(BLOCK, KD * BLOCK)  2.14 us
    unnamed x12, local copies, waits for them, and re-layouts  1.94 us
    transpose x1, local copies, waits for them, and re-layouts, shards(): jnp.transpose(inverse_table, (1, 0, 2)).reshape(BLOCK, KD * BLOCK)  1.7 us

profile of v1, /device:TPU:0, one launch (start us, length us, event | category | flops | bytes accessed | tf_op | source)
XLA Modules:
  0.0 51.9 jit_solution(5898090391346625394)
XLA Ops:
  0.0 0.0 copy-start.4
  0.0 1.0 %slice.7 = bf16[2,2,80,320]{3,2,1,0:T(8,128)(2,1)S(1)} slice(bf16[2,6,80,320]{3,2,1,0:T(8,128)(2,1)} %param.7), slice={[0:2], [0:2], [0:80], [0:320]} | slice | bytes 409600 | tf_op jit(solution)/shard_map/slice | solution.py:279
  1.1 0.2 copy.13.chain_ref
  1.3 0.0 copy-done.4
  1.3 0.0 copy-start.3
  1.3 0.1 slice.8
  1.3 0.1 copy.10
  1.4 0.2 copy.12.lat_ref
  1.6 0.8 %copy-done.3 = bf16[4,320,320]{2,1,0:T(8,128)(2,1)S(1)} copy-done((bf16[4,320,320]{2,1,0:T(8,128)(2,1)S(1)}, bf16[4,320,320]{2,1,0:T(8,128)(2,1)}, u32[]{:S(2)}) %copy-start.3) | copy-done | bytes 819224
  2.5 1.7 %copy.9 = bf16[320,4,320]{2,1,0:T(4,128)(2,1)} copy(bf16[320,4,320]{2,0,1:T(8,128)(2,1)S(1)} %bitcast.15) | data formatting | bytes 1638400 | tf_op jit(solution)/shard_map/transpose | solution.py:277
  4.2 0.0 copy-start
  4.2 0.0 copy-start.1
  4.2 0.0 copy-start.2
  4.2 2.1 %reshape.22.inv_ref = bf16[320,1280]{1,0:T(8,128)(2,1)S(1)} reshape(bf16[320,4,320]{2,1,0:T(4,128)(2,1)} %copy.9) | data formatting | bytes 1638400 | tf_op jit(solution)/shard_map/reshape | solution.py:277
  6.3 0.0 copy-done
  6.4 0.0 copy-done.1
  6.4 0.0 copy-done.2
  6.4 44.5 %shard_map.55 = f32[2560,128]{1,0:T(8,128)S(1)} custom-call(f32[2560,128]{1,0:T(8,128)S(1)} %bitcast.11, bf16[320,1280]{1,0:T(8,128)(2,1)S(1)} %reshape.22.inv_ref, bf16[320,640]{1,0:T(8,128)(2,1)S(1)} %copy.12.lat_ref, bf16[2,320,160]{2,1,0:T(8,128)(2,1)S(1)} %copy.13.chain_ref, s32[8,128]{1,0:T(8,128)S(1)} %bitcast.13, s32[6,8,128]{2,1,0:T(8,128)S(1)} %bitcast.12), custom_call_target="tpu_custom_call" | custom-call | tf_op jit(solution)/shard_map/pallas_call | solution.py:282
  50.8 1.1 %copy.16 = f32[1,320,8,128]{3,2,1,0:T(8,128)} copy(f32[1,320,8,128]{3,2,1,0:T(8,128)S(1)} %bitcast.10) | data formatting | bytes 2621440
  (1 shorter events, 0.0 us)
Async XLA Ops:
  0.0 1.3 %copy-start.4 = (bf16[2,6,80,320]{3,2,1,0:T(8,128)(2,1)S(1)}, bf16[2,6,80,320]{3,2,1,0:T(8,128)(2,1)}, u32[]{:S(2)}) copy-start(bf16[2,6,80,320]{3,2,1,0:T(8,128)(2,1)} %param.7) | copy-start | bytes 1843204
  1.3 1.2 %copy-start.3 = (bf16[4,320,320]{2,1,0:T(8,128)(2,1)S(1)}, bf16[4,320,320]{2,1,0:T(8,128)(2,1)}, u32[]{:S(2)}) copy-start(bf16[4,320,320]{2,1,0:T(8,128)(2,1)} %param.6) | copy-start | bytes 2457604
  4.2 2.2 %copy-start = (f32[1,320,8,128]{3,2,1,0:T(8,128)S(1)}, f32[1,320,8,128]{3,2,1,0:T(8,128)}, u32[]{:S(2)}) copy-start(f32[1,320,8,128]{3,2,1,0:T(8,128)} %param.5) | copy-start | bytes 3932164
  4.2 2.2 %copy-start.1 = (s32[1,6,8,128]{3,2,1,0:T(8,128)S(1)}, s32[1,6,8,128]{3,2,1,0:T(8,128)}, u32[]{:S(2)}) copy-start(s32[1,6,8,128]{3,2,1,0:T(8,128)} %param.9) | copy-start | bytes 73732
  4.2 2.2 %copy-start.2 = (s32[1,8,128]{2,1,0:T(8,128)S(1)}, s32[1,8,128]{2,1,0:T(8,128)}, u32[]{:S(2)}) copy-start(s32[1,8,128]{2,1,0:T(8,128)} %param.8) | copy-start | bytes 12292

commit v2 on v1

--- a/solution.py
+++ b/solution.py
@@ -15,6 +15,7 @@
 SWEEPS = 2
 HALVES = 2 * SWEEPS
 LANES = 128
+WIDE = 256
 GROUP = 4
 MESH = pl.DeviceIdType.MESH
 F32 = jnp.float32
@@ -24,12 +25,15 @@
 def kernel(
     rows,
     rhs_ref,
-    inv_ref,
-    lat_ref,
-    chain_ref,
+    table_ref,
+    coupling_ref,
     kind_ref,
     face_ref,
     out_ref,
+    inv_ref,
+    tall_ref,
+    lat_ref,
+    chain_ref,
     u_ref,
     base_ref,
     prod_ref,
@@ -78,6 +82,24 @@
                     barrier, inc=1, device_id=partner(name, step), device_id_type=MESH
                 )
 
+    for kind in range(KD):
+        inv_ref[:, kind * WIDE : (kind + 1) * WIDE] = table_ref[kind, :, :WIDE]
+    for pair in range(KD // 2):
+        inv_ref[:, KD * WIDE + pair * LANES : KD * WIDE + (pair + 1) * LANES] = jnp.concatenate(
+            [table_ref[2 * pair, :, WIDE:], table_ref[2 * pair + 1, :, WIDE:]], axis=1
+        )
+    for kind in range(KC):
+        tall_ref[kind * 4 * TRACE : (kind + 1) * 4 * TRACE, :BLOCK] = coupling_ref[
+            (kind * 6 + 2) * TRACE : (kind * 6 + 6) * TRACE, :
+        ]
+    lat_ref[...] = jnp.transpose(tall_ref[...])[:BLOCK]
+    for face in range(2):
+        for kind in range(KC):
+            tall_ref[kind * TRACE : (kind + 1) * TRACE, :BLOCK] = coupling_ref[
+                (kind * 6 + face) * TRACE : (kind * 6 + face + 1) * TRACE, :
+            ]
+        chain_ref[face] = jnp.transpose(tall_ref[: 2 * LANES, :])[:BLOCK, : KC * TRACE]
+
     pl.semaphore_wait(barrier, total)
 
     lane = lax.broadcasted_iota(jnp.int32, (TRACE, LANES), 1)
@@ -115,10 +137,10 @@
     def rhs_row(row):
         return rhs_ref[pl.ds(row, BLOCK, stride=rows), :]
 
-    def put_masked(stack, place, lanes, value, face, row):
+    def put_masked(stack, place, lanes, value, face, row, apart=TRACE):
         one = face_ref[face, row : row + 1, :].astype(F32)
         stack[pl.ds(place, TRACE), lanes] = value * (1.0 - one).astype(BF16)
-        stack[pl.ds(place + TRACE, TRACE), lanes] = value * one.astype(BF16)
+        stack[pl.ds(place + apart, TRACE), lanes] = value * one.astype(BF16)
 
     def edge_x(row, side):
         first = (NP - 1) * NP * side
@@ -139,27 +161,20 @@
                 from_xlow = edge_x(row - 1, 1).astype(BF16)
             else:
                 from_xlow = x_in[half, 0]
-            put_masked(lat_stack, 0, lanes, from_xlow, 2, row)
+            put_masked(lat_stack, 0, lanes, from_xlow, 2, row, 4 * TRACE)
             if row < rows - 1:
                 from_xhigh = edge_x(row + 1, 0).astype(BF16)
             else:
                 from_xhigh = x_in[half, 1]
-            put_masked(lat_stack, 2 * TRACE, lanes, from_xhigh, 3, row)
+            put_masked(lat_stack, TRACE, lanes, from_xhigh, 3, row, 4 * TRACE)
             seen = pltpu.roll(y_in[half, 0].astype(F32), (LANES - row) % LANES, 1)
             own = pltpu.roll(edge_y(row, 1), 1, 1)
-            put_masked(
-                lat_stack, 4 * TRACE, lanes, jnp.where(lane == 0, seen, own).astype(BF16), 4, row
-            )
+            from_ylow = jnp.where(lane == 0, seen, own).astype(BF16)
+            put_masked(lat_stack, 2 * TRACE, lanes, from_ylow, 4, row, 4 * TRACE)
             seen = pltpu.roll(y_in[half, 1].astype(F32), LANES - 1 - row, 1)
             own = pltpu.roll(edge_y(row, 0), LANES - 1, 1)
-            put_masked(
-                lat_stack,
-                6 * TRACE,
-                lanes,
-                jnp.where(lane == LANES - 1, seen, own).astype(BF16),
-                5,
-                row,
-            )
+            from_yhigh = jnp.where(lane == LANES - 1, seen, own).astype(BF16)
+            put_masked(lat_stack, 3 * TRACE, lanes, from_yhigh, 5, row, 4 * TRACE)
         product = jnp.dot(lat_ref[...], lat_stack[...], preferred_element_type=F32)
         for local in range(GROUP):
             row = group * GROUP + local
@@ -212,7 +227,10 @@
                 kinds = kind_ref[row : row + 1, :]
                 for kind in range(KD):
                     mask = jnp.where(kinds == kind, 1.0, 0.0).astype(BF16)
-                    inv_stack[kind * BLOCK : (kind + 1) * BLOCK, lanes] = residual * mask
+                    masked = residual * mask
+                    rest = KD * WIDE + kind * (BLOCK - WIDE)
+                    inv_stack[kind * WIDE : (kind + 1) * WIDE, lanes] = masked[:WIDE]
+                    inv_stack[rest : rest + BLOCK - WIDE, lanes] = masked[WIDE:]
             updated = jnp.dot(inv_ref[...], inv_stack[...], preferred_element_type=F32)
             for local in range(GROUP):
                 row = group * GROUP + local
@@ -274,17 +292,17 @@
     _, _, rows, width_y = right_side.shape
     groups = rows // GROUP
     columns = GROUP * LANES
-    inverse_wide = jnp.transpose(inverse_table, (1, 0, 2)).reshape(BLOCK, KD * BLOCK)
-    coupling_wide = jnp.transpose(coupling_table, (3, 1, 0, 2))
-    chain_wide = jnp.transpose(coupling_table[:, :2], (1, 3, 0, 2)).reshape(2, BLOCK, KC * TRACE)
-    lateral_wide = coupling_wide[:, 2:].reshape(BLOCK, 4 * KC * TRACE)
     vmem = pl.BlockSpec(memory_space=pltpu.VMEM)
     result = pl.pallas_call(
         functools.partial(kernel, rows),
         out_shape=jax.ShapeDtypeStruct((BLOCK * rows, LANES), F32),
-        in_specs=[vmem] * 6,
+        in_specs=[vmem] * 5,
         out_specs=vmem,
         scratch_shapes=[
+            pltpu.VMEM((BLOCK, KD * BLOCK), BF16),
+            pltpu.VMEM((4 * KC * TRACE, 3 * LANES), BF16),
+            pltpu.VMEM((BLOCK, 4 * KC * TRACE), BF16),
+            pltpu.VMEM((2, BLOCK, KC * TRACE), BF16),
             pltpu.VMEM((rows, BLOCK, LANES), F32),
             pltpu.VMEM((rows, BLOCK, LANES), F32),
             pltpu.VMEM((rows, BLOCK, LANES), F32),
@@ -310,9 +328,8 @@
         ),
     )(
         right_side.reshape(BLOCK * rows, width_y),
-        inverse_wide,
-        lateral_wide,
-        chain_wide,
+        inverse_table,
+        coupling_table.reshape(KC * 6 * TRACE, BLOCK),
         block_kind.reshape(rows, width_y),
         face_kind.reshape(6, rows, width_y),
     )

time: 52.1 us -> 50.9 us (0.977)
  local copies, waits for them, and re-layouts: 7.35 us -> 6.11 us
    unnamed x12 -> x11, local copies, waits for them, and re-layouts: 1.94 us -> 6.11 us
    reshape x3 -> x0, local copies, waits for them, and re-layouts: 2.56 us -> none  [the longest x1 2.14 us: shards(): jnp.transpose(inverse_table, (1, 0, 2)).reshape(BLOCK, KD * BLOCK)]
    transpose x1 -> x0, local copies, waits for them, and re-layouts: 1.7 us -> none  [shards(): jnp.transpose(inverse_table, (1, 0, 2)).reshape(BLOCK, KD * BLOCK)]
    slice x3 -> x0, local copies, waits for them, and re-layouts: 1.14 us -> none  [the longest x1 1.04 us: shards(): coupling_table[:, :2]]
where the time goes in v2:
time: 50.9 us; the launch traced here: 50.6 us
  Pallas kernels  44.5 us (87%)
  local copies, waits for them, and re-layouts  6.11 us (12%)
    pallas_call x1, Pallas kernels, shards(): pl.pallas_call(functools.partial(kernel, rows), out_shape=jax.ShapeDtypeS...  44.5 us
    unnamed x11, local copies, waits for them, and re-layouts  6.11 us

profile of v2, /device:TPU:0, one launch (start us, length us, event | category | flops | bytes accessed | tf_op | source)
XLA Modules:
  0.0 50.6 jit_solution(11660472286207183018)
XLA Ops:
  0.0 0.0 copy-start
  0.0 1.3 %copy-done = f32[1,320,8,128]{3,2,1,0:T(8,128)S(1)} copy-done((f32[1,320,8,128]{3,2,1,0:T(8,128)S(1)}, f32[1,320,8,128]{3,2,1,0:T(8,128)}, u32[]{:S(2)}) %copy-start) | copy-done | bytes 1310744
  1.3 0.0 copy-start.1
  1.3 1.2 %copy-done.1 = bf16[4,320,320]{2,1,0:T(8,128)(2,1)S(1)} copy-done((bf16[4,320,320]{2,1,0:T(8,128)(2,1)S(1)}, bf16[4,320,320]{2,1,0:T(8,128)(2,1)}, u32[]{:S(2)}) %copy-start.1) | copy-done | bytes 819224
  2.5 0.0 copy-start.2
  2.5 1.1 %copy-done.2 = bf16[2,6,80,320]{3,2,1,0:T(8,128)(2,1)S(1)} copy-done((bf16[2,6,80,320]{3,2,1,0:T(8,128)(2,1)S(1)}, bf16[2,6,80,320]{3,2,1,0:T(8,128)(2,1)}, u32[]{:S(2)}) %copy-start.2) | copy-done | bytes 614424
  3.6 0.0 copy-start.3
  3.6 0.7 %copy-done.3 = s32[1,6,8,128]{3,2,1,0:T(8,128)S(1)} copy-done((s32[1,6,8,128]{3,2,1,0:T(8,128)S(1)}, s32[1,6,8,128]{3,2,1,0:T(8,128)}, u32[]{:S(2)}) %copy-start.3) | copy-done | bytes 24600
  4.4 0.0 copy-start.4
  4.4 0.7 %copy-done.4 = s32[1,8,128]{2,1,0:T(8,128)S(1)} copy-done((s32[1,8,128]{2,1,0:T(8,128)S(1)}, s32[1,8,128]{2,1,0:T(8,128)}, u32[]{:S(2)}) %copy-start.4) | copy-done | bytes 4120
  5.1 44.5 %shard_map.55 = f32[2560,128]{1,0:T(8,128)S(1)} custom-call(f32[2560,128]{1,0:T(8,128)S(1)} %bitcast.6, bf16[4,320,320]{2,1,0:T(8,128)(2,1)S(1)} %copy-done.1, bf16[960,320]{1,0:T(8,128)(2,1)S(1)} %bitcast.7, s32[8,128]{1,0:T(8,128)S(1)} %bitcast.9, s32[6,8,128]{2,1,0:T(8,128)S(1)} %bitcast.8), custom_call_target="tpu_custom_call" | custom-call | tf_op jit(solution)/shard_map/pallas_call | solution.py:296
  49.6 1.1 %copy.7 = f32[1,320,8,128]{3,2,1,0:T(8,128)} copy(f32[1,320,8,128]{3,2,1,0:T(8,128)S(1)} %bitcast.5) | data formatting | bytes 2621440
Async XLA Ops:
  0.0 1.3 %copy-start = (f32[1,320,8,128]{3,2,1,0:T(8,128)S(1)}, f32[1,320,8,128]{3,2,1,0:T(8,128)}, u32[]{:S(2)}) copy-start(f32[1,320,8,128]{3,2,1,0:T(8,128)} %param.5) | copy-start | bytes 3932164
  1.3 1.2 %copy-start.1 = (bf16[4,320,320]{2,1,0:T(8,128)(2,1)S(1)}, bf16[4,320,320]{2,1,0:T(8,128)(2,1)}, u32[]{:S(2)}) copy-start(bf16[4,320,320]{2,1,0:T(8,128)(2,1)} %table_ref.1) | copy-start | bytes 2457604
  2.5 1.1 %copy-start.2 = (bf16[2,6,80,320]{3,2,1,0:T(8,128)(2,1)S(1)}, bf16[2,6,80,320]{3,2,1,0:T(8,128)(2,1)}, u32[]{:S(2)}) copy-start(bf16[2,6,80,320]{3,2,1,0:T(8,128)(2,1)} %param.7) | copy-start | bytes 1843204
  3.6 0.7 %copy-start.3 = (s32[1,6,8,128]{3,2,1,0:T(8,128)S(1)}, s32[1,6,8,128]{3,2,1,0:T(8,128)}, u32[]{:S(2)}) copy-start(s32[1,6,8,128]{3,2,1,0:T(8,128)} %param.9) | copy-start | bytes 73732
  4.4 0.7 %copy-start.4 = (s32[1,8,128]{2,1,0:T(8,128)S(1)}, s32[1,8,128]{2,1,0:T(8,128)}, u32[]{:S(2)}) copy-start(s32[1,8,128]{2,1,0:T(8,128)} %param.8) | copy-start | bytes 12292

commit v3 on v2

v3 whole, which is shorter than its diff:
```python
import functools
import jax
import jax.numpy as jnp
from jax import lax
from jax.experimental import pallas as pl
from jax.experimental.pallas import tpu as pltpu
from jax.sharding import PartitionSpec as P

NVAR = 5
NP = 4
BLOCK = 320
TRACE = 80
KD = 4
KC = 2
SWEEPS = 2
HALVES = 2 * SWEEPS
LANES = 128
WIDE = 256
GROUP = 2
MESH = pl.DeviceIdType.MESH
F32 = jnp.float32
BF16 = jnp.bfloat16


def kernel(
    rows,
    rhs_ref,
    table_ref,
    coupling_ref,
    kind_ref,
    face_ref,
    out_ref,
    inv_ref,
    tall_ref,
    lat_ref,
    chain_ref,
    u_ref,
    base_ref,
    prod_ref,
    tr_ref,
    lat_stack,
    chain_stack,
    inv_stack,
    front_in,
    front_out,
    x_low,
    x_high,
    y_in,
    y_out,
    front_send,
    front_recv,
    x_send,
    x_recv,
    y_send,
    y_recv,
):
    groups = rows // GROUP
    places = {}
    for name in ("sweep", "cx", "cy"):
        places[name] = (lax.axis_index(name), lax.axis_size(name))

    def has(name, step):
        spot, count = places[name]
        return spot < count - 1 if step > 0 else spot > 0

    def partner(name, step):
        return {name: places[name][0] + step}

    for half in range(HALVES - 1):
        x_high[half, 0] = jnp.zeros((TRACE, LANES), BF16)
        x_low[half, rows + 1] = jnp.zeros((TRACE, LANES), BF16)
    for side in range(2):

        @pl.when(jnp.logical_not(has("cy", 2 * side - 1)))
        def _():
            for half in range(HALVES - 1):
                y_in[half, side] = jnp.zeros((groups, TRACE, LANES), BF16)

    barrier = pltpu.get_barrier_semaphore()
    total = 0
    for name in ("sweep", "cx", "cy"):
        for step in (-1, 1):
            exists = has(name, step)
            total = total + jnp.where(exists, 1, 0)

            @pl.when(exists)
            def _():
                pl.semaphore_signal(
                    barrier, inc=1, device_id=partner(name, step), device_id_type=MESH
                )

    for kind in range(KD):
        inv_ref[:, kind * WIDE : (kind + 1) * WIDE] = table_ref[kind, :, :WIDE]
    for pair in range(KD // 2):
        inv_ref[:, KD * WIDE + pair * LANES : KD * WIDE + (pair + 1) * LANES] = jnp.concatenate(
            [table_ref[2 * pair, :, WIDE:], table_ref[2 * pair + 1, :, WIDE:]], axis=1
        )
    pl.semaphore_wait(barrier, total)

    def lay_out_coupling():
        for kind in range(KC):
            tall_ref[kind * 4 * TRACE : (kind + 1) * 4 * TRACE, :BLOCK] = coupling_ref[
                (kind * 6 + 2) * TRACE : (kind * 6 + 6) * TRACE, :
            ]
        lat_ref[...] = jnp.transpose(tall_ref[...])[:BLOCK]
        for face in range(2):
            for kind in range(KC):
                tall_ref[kind * TRACE : (kind + 1) * TRACE, :BLOCK] = coupling_ref[
                    (kind * 6 + face) * TRACE : (kind * 6 + face + 1) * TRACE, :
                ]
            chain_ref[face] = jnp.transpose(tall_ref[: 2 * LANES, :])[:BLOCK, : KC * TRACE]

    lane = lax.broadcasted_iota(jnp.int32, (TRACE, LANES), 1)
    flip = lax.rem(places["cx"][0], 2)

    def place_of(turn):
        return turn + flip * (groups - 1 - 2 * turn)

    def front_copy(half, group, step):
        return pltpu.make_async_remote_copy(
            src_ref=front_out.at[half, group],
            dst_ref=front_in.at[half, group],
            send_sem=front_send.at[half, group],
            recv_sem=front_recv.at[half, group],
            device_id=partner("sweep", step),
            device_id_type=MESH,
        )

    def x_copy(half, side):
        source, target = (x_low.at[half, 1], x_low.at[half, rows + 1])
        if side == 1:
            source, target = (x_high.at[half, rows], x_high.at[half, 0])
        return pltpu.make_async_remote_copy(
            src_ref=source,
            dst_ref=target,
            send_sem=x_send.at[half, side],
            recv_sem=x_recv.at[half, 1 - side],
            device_id=partner("cx", 2 * side - 1),
            device_id_type=MESH,
        )

    def y_copy(half, side, group):
        return pltpu.make_async_remote_copy(
            src_ref=y_out.at[half, side, group],
            dst_ref=y_in.at[half, 1 - side, group],
            send_sem=y_send.at[half, side, group],
            recv_sem=y_recv.at[half, 1 - side, group],
            device_id=partner("cy", 2 * side - 1),
            device_id_type=MESH,
        )

    def x_here(side, group):
        return jnp.logical_and(has("cx", 2 * side - 1), group == (groups - 1) * side)

    def rhs_row(row):
        return rhs_ref[pl.ds(row, BLOCK, stride=rows), :]

    def put_masked(stack, place, lanes, value, face, row, apart):
        one = face_ref[face, pl.ds(row, 1), :].astype(F32)
        stack[place : place + TRACE, lanes] = value * (1.0 - one).astype(BF16)
        stack[place + apart : place + apart + TRACE, lanes] = value * one.astype(BF16)

    def edge_x(row, local, side):
        first = (NP - 1) * NP * side
        for node in range(NP):
            tr_ref[local, side, pl.ds(node, NVAR * NP, stride=NP), :] = u_ref[
                row, pl.ds(first + node, NVAR * NP, stride=NP * NP), :
            ]
        return tr_ref[local, side].astype(BF16)

    def edge_y(row, side):
        return u_ref[row, pl.ds((NP - 1) * side, TRACE, stride=NP), :]

    def turned(value, shift):
        return pltpu.roll(value, shift % LANES, 1) if shift % LANES else value

    def lateral(half, group):
        for side in range(2):

            @pl.when(x_here(side, group))
            def _():
                x_copy(half, 1 - side).wait_recv()

            @pl.when(has("cy", 2 * side - 1))
            def _():
                y_copy(half, 1 - side, group).wait_recv()

        for local in range(GROUP):
            row = group * GROUP + local
            lanes = slice(local * LANES, (local + 1) * LANES)
            apart = 4 * TRACE
            put_masked(lat_stack, 0, lanes, x_high[half, row], 2, row, apart)
            put_masked(lat_stack, TRACE, lanes, x_low[half, row + 2], 3, row, apart)
            seen = turned(y_in[half, 0, group].astype(F32), -local)
            from_ylow = jnp.where(lane == 0, seen, turned(edge_y(row, 1), 1))
            put_masked(lat_stack, 2 * TRACE, lanes, from_ylow.astype(BF16), 4, row, apart)
            seen = turned(y_in[half, 1, group].astype(F32), -1 - local)
            from_yhigh = jnp.where(lane == LANES - 1, seen, turned(edge_y(row, 0), -1))
            put_masked(lat_stack, 3 * TRACE, lanes, from_yhigh.astype(BF16), 5, row, apart)
        product = jnp.dot(lat_ref[...], lat_stack[...], preferred_element_type=F32)
        for local in range(GROUP):
            row = group * GROUP + local
            lanes = slice(local * LANES, (local + 1) * LANES)
            base_ref[row] = rhs_row(row) - product[:, lanes] - prod_ref[row]

    def update(half, group, upstream, downstream):
        forward = half % 2 == 0
        step = 1 if forward else -1

        @pl.when(upstream)
        def _():
            front_copy(half, group, step).wait_recv()
            face = 0 if forward else 1
            for local in range(GROUP):
                row = group * GROUP + local
                lanes = slice(local * LANES, (local + 1) * LANES)
                put_masked(
                    chain_stack, 0, lanes, front_in[half, group, local], face, row, TRACE
                )
            product = jnp.dot(chain_ref[face], chain_stack[...], preferred_element_type=F32)
            for local in range(GROUP):
                row = group * GROUP + local
                part = product[:, local * LANES : (local + 1) * LANES]
                prod_ref[row] = part
                base_ref[row] = (rhs_row(row) if half == 0 else base_ref[row]) - part

        @pl.when(jnp.logical_not(upstream))
        def _():
            for local in range(GROUP):
                row = group * GROUP + local
                prod_ref[row] = jnp.zeros((BLOCK, LANES), F32)
                if half == 0:
                    base_ref[row] = rhs_row(row)

        for local in range(GROUP):
            row = group * GROUP + local
            lanes = slice(local * LANES, (local + 1) * LANES)
            residual = base_ref[row].astype(BF16)
            kinds = kind_ref[pl.ds(row, 1), :]
            for kind in range(KD):
                masked = residual * jnp.where(kinds == kind, 1.0, 0.0).astype(BF16)
                rest = KD * WIDE + kind * (BLOCK - WIDE)
                inv_stack[kind * WIDE : (kind + 1) * WIDE, lanes] = masked[:WIDE]
                inv_stack[rest : rest + BLOCK - WIDE, lanes] = masked[WIDE:]
        updated = jnp.dot(inv_ref[...], inv_stack[...], preferred_element_type=F32)
        first = NP * NP * (NP - 1) if forward else 0
        for local in range(GROUP):
            value = updated[:, local * LANES : (local + 1) * LANES]
            for var in range(NVAR):
                start = var * NP * NP * NP + first
                front_out[half, group, local, var * NP * NP : (var + 1) * NP * NP, :] = value[
                    start : start + NP * NP, :
                ].astype(BF16)

        @pl.when(downstream)
        def _():
            front_copy(half, group, step).start()

        for local in range(GROUP):
            row = group * GROUP + local
            value = updated[:, local * LANES : (local + 1) * LANES]
            if half == HALVES - 1:
                out_ref[pl.ds(row, BLOCK, stride=rows), :] = value
            else:
                u_ref[row] = value
        if half == HALVES - 1:
            return
        for side in range(2):
            first_row = edge_y(group * GROUP, side)
            packed = turned(first_row, side)
            for local in range(1, GROUP):
                other = turned(edge_y(group * GROUP + local, side), local + side)
                packed = jnp.where(lane == local, other, packed)
            y_out[half, side, group] = packed.astype(BF16)

            @pl.when(has("cy", 2 * side - 1))
            def _():
                y_copy(half, side, group).start()

        for local in range(GROUP):
            row = group * GROUP + local
            x_low[half, row + 1] = edge_x(row, local, 0)
            x_high[half, row + 1] = edge_x(row, local, 1)
        for side in range(2):

            @pl.when(x_here(side, group))
            def _():
                x_copy(half, side).start()

    for half in range(HALVES):
        step = 1 if half % 2 == 0 else -1
        upstream = has("sweep", -step)
        downstream = has("sweep", step)

        @pl.when(upstream)
        def _():
            if half == 0:
                lay_out_coupling()
            else:

                @pl.loop(0, groups)
                def _(turn):
                    lateral(half - 1, place_of(turn))

        @pl.loop(0, groups)
        def _(turn):
            group = place_of(turn)
            if half > 0:

                @pl.when(jnp.logical_not(upstream))
                def _():
                    lateral(half - 1, group)

            update(half, group, upstream, downstream)

        if half == 0:

            @pl.when(jnp.logical_not(upstream))
            def _():
                lay_out_coupling()

    for half in range(HALVES):
        step = 1 if half % 2 == 0 else -1

        @pl.when(has("sweep", step))
        def _():
            @pl.loop(0, groups)
            def _(group):
                front_copy(half, group, step).wait_send()

        if half < HALVES - 1:
            for side in range(2):

                @pl.when(has("cy", 2 * side - 1))
                def _():
                    @pl.loop(0, groups)
                    def _(group):
                        y_copy(half, side, group).wait_send()

                @pl.when(has("cx", 2 * side - 1))
                def _():
                    x_copy(half, side).wait_send()


def shards(right_side, inverse_table, coupling_table, block_kind, face_kind):
    _, _, rows, width_y = right_side.shape
    groups = rows // GROUP
    columns = GROUP * LANES
    vmem = pl.BlockSpec(memory_space=pltpu.VMEM)
    result = pl.pallas_call(
        functools.partial(kernel, rows),
        out_shape=jax.ShapeDtypeStruct((BLOCK * rows, LANES), F32),
        in_specs=[vmem] * 5,
        out_specs=vmem,
        scratch_shapes=[
            pltpu.VMEM((BLOCK, KD * BLOCK), BF16),
            pltpu.VMEM((4 * KC * TRACE, 3 * LANES), BF16),
            pltpu.VMEM((BLOCK, 4 * KC * TRACE), BF16),
            pltpu.VMEM((2, BLOCK, KC * TRACE), BF16),
            pltpu.VMEM((rows, BLOCK, LANES), F32),
            pltpu.VMEM((rows, BLOCK, LANES), F32),
            pltpu.VMEM((rows, BLOCK, LANES), F32),
            pltpu.VMEM((GROUP, 2, TRACE, LANES), F32),
            pltpu.VMEM((4 * KC * TRACE, columns), BF16),
            pltpu.VMEM((KC * TRACE, columns), BF16),
            pltpu.VMEM((KD * BLOCK, columns), BF16),
            pltpu.VMEM((HALVES, groups, GROUP, TRACE, LANES), BF16),
            pltpu.VMEM((HALVES, groups, GROUP, TRACE, LANES), BF16),
            pltpu.VMEM((HALVES - 1, rows + 2, TRACE, LANES), BF16),
            pltpu.VMEM((HALVES - 1, rows + 2, TRACE, LANES), BF16),
            pltpu.VMEM((HALVES - 1, 2, groups, TRACE, LANES), BF16),
            pltpu.VMEM((HALVES - 1, 2, groups, TRACE, LANES), BF16),
            pltpu.SemaphoreType.DMA((HALVES, groups)),
            pltpu.SemaphoreType.DMA((HALVES, groups)),
            pltpu.SemaphoreType.DMA((HALVES - 1, 2)),
            pltpu.SemaphoreType.DMA((HALVES - 1, 2)),
            pltpu.SemaphoreType.DMA((HALVES - 1, 2, groups)),
            pltpu.SemaphoreType.DMA((HALVES - 1, 2, groups)),
        ],
        compiler_params=pltpu.CompilerParams(
            collective_id=0, has_side_effects=True, vmem_limit_bytes=48 << 20
        ),
    )(
        right_side.reshape(BLOCK * rows, width_y),
        inverse_table,
        coupling_table.reshape(KC * 6 * TRACE, BLOCK),
        block_kind.reshape(rows, width_y),
        face_kind.reshape(6, rows, width_y),
    )
    return result.reshape(right_side.shape)


def solution(mesh):
    in_specs = (
        P("sweep", None, "cx", "cy"),
        P(),
        P(),
        P("sweep", "cx", "cy"),
        P("sweep", None, "cx", "cy"),
    )
    out_specs = P("sweep", None, "cx", "cy")
    return jax.shard_map(shards, mesh=mesh, in_specs=in_specs, out_specs=out_specs, check_vma=False)
```

time: 50.9 us -> 42.8 us (0.84)
  Pallas kernels: 44.5 us -> 36.3 us
    pallas_call x1, Pallas kernels: 44.5 us -> 36.3 us  [shards(): pl.pallas_call(functools.partial(kernel, rows), out_shape=jax.ShapeDtypeS...]
where the time goes in v3:
time: 42.8 us; the launch traced here: 42.4 us
  Pallas kernels  36.3 us (85%)
  local copies, waits for them, and re-layouts  6.11 us (14%)
    pallas_call x1, Pallas kernels, shards(): pl.pallas_call(functools.partial(kernel, rows), out_shape=jax.ShapeDtypeS...  36.3 us
    unnamed x11, local copies, waits for them, and re-layouts  6.11 us

profile of v3, /device:TPU:0, one launch (start us, length us, event | category | flops | bytes accessed | tf_op | source)
XLA Modules:
  0.0 42.4 jit_solution(11961298075191955547)
XLA Ops:
  0.0 0.0 copy-start
  0.0 1.3 %copy-done = f32[1,320,8,128]{3,2,1,0:T(8,128)S(1)} copy-done((f32[1,320,8,128]{3,2,1,0:T(8,128)S(1)}, f32[1,320,8,128]{3,2,1,0:T(8,128)}, u32[]{:S(2)}) %copy-start) | copy-done | bytes 1310744
  1.3 0.0 copy-start.1
  1.3 1.2 %copy-done.1 = bf16[4,320,320]{2,1,0:T(8,128)(2,1)S(1)} copy-done((bf16[4,320,320]{2,1,0:T(8,128)(2,1)S(1)}, bf16[4,320,320]{2,1,0:T(8,128)(2,1)}, u32[]{:S(2)}) %copy-start.1) | copy-done | bytes 819224
  2.5 0.0 copy-start.2
  2.5 1.1 %copy-done.2 = bf16[2,6,80,320]{3,2,1,0:T(8,128)(2,1)S(1)} copy-done((bf16[2,6,80,320]{3,2,1,0:T(8,128)(2,1)S(1)}, bf16[2,6,80,320]{3,2,1,0:T(8,128)(2,1)}, u32[]{:S(2)}) %copy-start.2) | copy-done | bytes 614424
  3.6 0.0 copy-start.3
  3.6 0.7 %copy-done.3 = s32[1,6,8,128]{3,2,1,0:T(8,128)S(1)} copy-done((s32[1,6,8,128]{3,2,1,0:T(8,128)S(1)}, s32[1,6,8,128]{3,2,1,0:T(8,128)}, u32[]{:S(2)}) %copy-start.3) | copy-done | bytes 24600
  4.4 0.0 copy-start.4
  4.4 0.7 %copy-done.4 = s32[1,8,128]{2,1,0:T(8,128)S(1)} copy-done((s32[1,8,128]{2,1,0:T(8,128)S(1)}, s32[1,8,128]{2,1,0:T(8,128)}, u32[]{:S(2)}) %copy-start.4) | copy-done | bytes 4120
  5.1 36.3 %shard_map.55 = f32[2560,128]{1,0:T(8,128)S(1)} custom-call(f32[2560,128]{1,0:T(8,128)S(1)} %bitcast.6, bf16[4,320,320]{2,1,0:T(8,128)(2,1)S(1)} %copy-done.1, bf16[960,320]{1,0:T(8,128)(2,1)S(1)} %bitcast.7, s32[8,128]{1,0:T(8,128)S(1)} %bitcast.9, s32[6,8,128]{2,1,0:T(8,128)S(1)} %bitcast.8), custom_call_target="tpu_custom_call" | custom-call | tf_op jit(solution)/shard_map/pallas_call | solution.py:350
  41.4 1.1 %copy.7 = f32[1,320,8,128]{3,2,1,0:T(8,128)} copy(f32[1,320,8,128]{3,2,1,0:T(8,128)S(1)} %bitcast.5) | data formatting | bytes 2621440
Async XLA Ops:
  0.0 1.3 %copy-start = (f32[1,320,8,128]{3,2,1,0:T(8,128)S(1)}, f32[1,320,8,128]{3,2,1,0:T(8,128)}, u32[]{:S(2)}) copy-start(f32[1,320,8,128]{3,2,1,0:T(8,128)} %param.5) | copy-start | bytes 3932164
  1.3 1.2 %copy-start.1 = (bf16[4,320,320]{2,1,0:T(8,128)(2,1)S(1)}, bf16[4,320,320]{2,1,0:T(8,128)(2,1)}, u32[]{:S(2)}) copy-start(bf16[4,320,320]{2,1,0:T(8,128)(2,1)} %table_ref.1) | copy-start | bytes 2457604
  2.5 1.1 %copy-start.2 = (bf16[2,6,80,320]{3,2,1,0:T(8,128)(2,1)S(1)}, bf16[2,6,80,320]{3,2,1,0:T(8,128)(2,1)}, u32[]{:S(2)}) copy-start(bf16[2,6,80,320]{3,2,1,0:T(8,128)(2,1)} %param.7) | copy-start | bytes 1843204
  3.6 0.7 %copy-start.3 = (s32[1,6,8,128]{3,2,1,0:T(8,128)S(1)}, s32[1,6,8,128]{3,2,1,0:T(8,128)}, u32[]{:S(2)}) copy-start(s32[1,6,8,128]{3,2,1,0:T(8,128)} %param.9) | copy-start | bytes 73732
  4.4 0.7 %copy-start.4 = (s32[1,8,128]{2,1,0:T(8,128)S(1)}, s32[1,8,128]{2,1,0:T(8,128)}, u32[]{:S(2)}) copy-start(s32[1,8,128]{2,1,0:T(8,128)} %param.8) | copy-start | bytes 12292

commit v4 on v3

--- a/solution.py
+++ b/solution.py
@@ -24,22 +24,25 @@
 
 def kernel(
     rows,
+    rhs_in,
+    table_in,
+    coupling_in,
+    kind_in,
+    face_in,
+    out_ref,
     rhs_ref,
     table_ref,
     coupling_ref,
     kind_ref,
     face_ref,
-    out_ref,
+    load_sem,
     inv_ref,
     tall_ref,
-    lat_ref,
-    chain_ref,
+    wide_ref,
     u_ref,
-    base_ref,
-    prod_ref,
+    res_ref,
     tr_ref,
-    lat_stack,
-    chain_stack,
+    stack,
     inv_stack,
     front_in,
     front_out,
@@ -55,6 +58,20 @@
     y_recv,
 ):
     groups = rows // GROUP
+    loads = [
+        pltpu.make_async_copy(source, target, load_sem.at[spot])
+        for spot, (source, target) in enumerate(
+            (
+                (table_in, table_ref),
+                (rhs_in, rhs_ref),
+                (kind_in, kind_ref),
+                (coupling_in, coupling_ref),
+                (face_in, face_ref),
+            )
+        )
+    ]
+    for load in loads:
+        load.start()
     places = {}
     for name in ("sweep", "cx", "cy"):
         places[name] = (lax.axis_index(name), lax.axis_size(name))
@@ -89,26 +106,21 @@
                     barrier, inc=1, device_id=partner(name, step), device_id_type=MESH
                 )
 
+    stack[...] = jnp.zeros(stack.shape, BF16)
+    loads[0].wait()
     for kind in range(KD):
         inv_ref[:, kind * WIDE : (kind + 1) * WIDE] = table_ref[kind, :, :WIDE]
     for pair in range(KD // 2):
         inv_ref[:, KD * WIDE + pair * LANES : KD * WIDE + (pair + 1) * LANES] = jnp.concatenate(
             [table_ref[2 * pair, :, WIDE:], table_ref[2 * pair + 1, :, WIDE:]], axis=1
         )
+    for load in loads[1:]:
+        load.wait()
     pl.semaphore_wait(barrier, total)
 
     def lay_out_coupling():
-        for kind in range(KC):
-            tall_ref[kind * 4 * TRACE : (kind + 1) * 4 * TRACE, :BLOCK] = coupling_ref[
-                (kind * 6 + 2) * TRACE : (kind * 6 + 6) * TRACE, :
-            ]
-        lat_ref[...] = jnp.transpose(tall_ref[...])[:BLOCK]
-        for face in range(2):
-            for kind in range(KC):
-                tall_ref[kind * TRACE : (kind + 1) * TRACE, :BLOCK] = coupling_ref[
-                    (kind * 6 + face) * TRACE : (kind * 6 + face + 1) * TRACE, :
-                ]
-            chain_ref[face] = jnp.transpose(tall_ref[: 2 * LANES, :])[:BLOCK, : KC * TRACE]
+        tall_ref[: KC * 6 * TRACE, :BLOCK] = coupling_ref[...]
+        wide_ref[...] = jnp.transpose(tall_ref[...])[:BLOCK, : KC * 6 * TRACE]
 
     lane = lax.broadcasted_iota(jnp.int32, (TRACE, LANES), 1)
     flip = lax.rem(places["cx"][0], 2)
@@ -155,10 +167,12 @@
     def rhs_row(row):
         return rhs_ref[pl.ds(row, BLOCK, stride=rows), :]
 
-    def put_masked(stack, place, lanes, value, face, row, apart):
+    def put_masked(group, lanes, value, face, row):
         one = face_ref[face, pl.ds(row, 1), :].astype(F32)
-        stack[place : place + TRACE, lanes] = value * (1.0 - one).astype(BF16)
-        stack[place + apart : place + apart + TRACE, lanes] = value * one.astype(BF16)
+        place = face * TRACE
+        stack[group, place : place + TRACE, lanes] = value * (1.0 - one).astype(BF16)
+        place = (6 + face) * TRACE
+        stack[group, place : place + TRACE, lanes] = value * one.astype(BF16)
 
     def edge_x(row, local, side):
         first = (NP - 1) * NP * side
@@ -188,24 +202,25 @@
         for local in range(GROUP):
             row = group * GROUP + local
             lanes = slice(local * LANES, (local + 1) * LANES)
-            apart = 4 * TRACE
-            put_masked(lat_stack, 0, lanes, x_high[half, row], 2, row, apart)
-            put_masked(lat_stack, TRACE, lanes, x_low[half, row + 2], 3, row, apart)
+            put_masked(group, lanes, x_high[half, row], 2, row)
+            put_masked(group, lanes, x_low[half, row + 2], 3, row)
             seen = turned(y_in[half, 0, group].astype(F32), -local)
             from_ylow = jnp.where(lane == 0, seen, turned(edge_y(row, 1), 1))
-            put_masked(lat_stack, 2 * TRACE, lanes, from_ylow.astype(BF16), 4, row, apart)
+            put_masked(group, lanes, from_ylow.astype(BF16), 4, row)
             seen = turned(y_in[half, 1, group].astype(F32), -1 - local)
             from_yhigh = jnp.where(lane == LANES - 1, seen, turned(edge_y(row, 0), -1))
-            put_masked(lat_stack, 3 * TRACE, lanes, from_yhigh.astype(BF16), 5, row, apart)
-        product = jnp.dot(lat_ref[...], lat_stack[...], preferred_element_type=F32)
-        for local in range(GROUP):
-            row = group * GROUP + local
-            lanes = slice(local * LANES, (local + 1) * LANES)
-            base_ref[row] = rhs_row(row) - product[:, lanes] - prod_ref[row]
+            put_masked(group, lanes, from_yhigh.astype(BF16), 5, row)
 
     def update(half, group, upstream, downstream):
         forward = half % 2 == 0
         step = 1 if forward else -1
+
+        def coupled():
+            product = jnp.dot(wide_ref[...], stack[group], preferred_element_type=F32)
+            for local in range(GROUP):
+                row = group * GROUP + local
+                part = product[:, local * LANES : (local + 1) * LANES]
+                res_ref[local] = (rhs_row(row) - part).astype(BF16)
 
         @pl.when(upstream)
         def _():
@@ -214,28 +229,24 @@
             for local in range(GROUP):
                 row = group * GROUP + local
                 lanes = slice(local * LANES, (local + 1) * LANES)
-                put_masked(
-                    chain_stack, 0, lanes, front_in[half, group, local], face, row, TRACE
-                )
-            product = jnp.dot(chain_ref[face], chain_stack[...], preferred_element_type=F32)
-            for local in range(GROUP):
-                row = group * GROUP + local
-                part = product[:, local * LANES : (local + 1) * LANES]
-                prod_ref[row] = part
-                base_ref[row] = (rhs_row(row) if half == 0 else base_ref[row]) - part
-
-        @pl.when(jnp.logical_not(upstream))
-        def _():
-            for local in range(GROUP):
-                row = group * GROUP + local
-                prod_ref[row] = jnp.zeros((BLOCK, LANES), F32)
-                if half == 0:
-                    base_ref[row] = rhs_row(row)
+                put_masked(group, lanes, front_in[half, group, local], face, row)
+            if half == 0:
+                coupled()
+
+        if half == 0:
+
+            @pl.when(jnp.logical_not(upstream))
+            def _():
+                for local in range(GROUP):
+                    res_ref[local] = rhs_row(group * GROUP + local).astype(BF16)
+
+        else:
+            coupled()
 
         for local in range(GROUP):
             row = group * GROUP + local
             lanes = slice(local * LANES, (local + 1) * LANES)
-            residual = base_ref[row].astype(BF16)
+            residual = res_ref[local]
             kinds = kind_ref[pl.ds(row, 1), :]
             for kind in range(KD):
                 masked = residual * jnp.where(kinds == kind, 1.0, 0.0).astype(BF16)
@@ -347,22 +358,27 @@
     groups = rows // GROUP
     columns = GROUP * LANES
     vmem = pl.BlockSpec(memory_space=pltpu.VMEM)
+    hbm = pl.BlockSpec(memory_space=pltpu.HBM)
+    inputs = KC * 6 * TRACE
     result = pl.pallas_call(
         functools.partial(kernel, rows),
         out_shape=jax.ShapeDtypeStruct((BLOCK * rows, LANES), F32),
-        in_specs=[vmem] * 5,
+        in_specs=[hbm] * 5,
         out_specs=vmem,
         scratch_shapes=[
+            pltpu.VMEM((BLOCK * rows, LANES), F32),
+            pltpu.VMEM((KD, BLOCK, BLOCK), BF16),
+            pltpu.VMEM((inputs, BLOCK), BF16),
+            pltpu.VMEM((rows, LANES), jnp.int32),
+            pltpu.VMEM((6, rows, LANES), jnp.int32),
+            pltpu.SemaphoreType.DMA((5,)),
             pltpu.VMEM((BLOCK, KD * BLOCK), BF16),
-            pltpu.VMEM((4 * KC * TRACE, 3 * LANES), BF16),
-            pltpu.VMEM((BLOCK, 4 * KC * TRACE), BF16),
-            pltpu.VMEM((2, BLOCK, KC * TRACE), BF16),
+            pltpu.VMEM((8 * LANES, 3 * LANES), BF16),
+            pltpu.VMEM((BLOCK, inputs), BF16),
             pltpu.VMEM((rows, BLOCK, LANES), F32),
-            pltpu.VMEM((rows, BLOCK, LANES), F32),
-            pltpu.VMEM((rows, BLOCK, LANES), F32),
+            pltpu.VMEM((GROUP, BLOCK, LANES), BF16),
             pltpu.VMEM((GROUP, 2, TRACE, LANES), F32),
-            pltpu.VMEM((4 * KC * TRACE, columns), BF16),
-            pltpu.VMEM((KC * TRACE, columns), BF16),
+            pltpu.VMEM((groups, inputs, columns), BF16),
             pltpu.VMEM((KD * BLOCK, columns), BF16),
             pltpu.VMEM((HALVES, groups, GROUP, TRACE, LANES), BF16),
             pltpu.VMEM((HALVES, groups, GROUP, TRACE, LANES), BF16),
@@ -378,12 +394,12 @@
             pltpu.SemaphoreType.DMA((HALVES - 1, 2, groups)),
         ],
         compiler_params=pltpu.CompilerParams(
-            collective_id=0, has_side_effects=True, vmem_limit_bytes=48 << 20
+            collective_id=0, has_side_effects=True, vmem_limit_bytes=62 << 20
         ),
     )(
         right_side.reshape(BLOCK * rows, width_y),
         inverse_table,
-        coupling_table.reshape(KC * 6 * TRACE, BLOCK),
+        coupling_table.reshape(inputs, BLOCK),
         block_kind.reshape(rows, width_y),
         face_kind.reshape(6, rows, width_y),
     )

time: 42.8 us -> 45 us (1.051)
  Pallas kernels: 36.3 us -> 42.4 us
  local copies, waits for them, and re-layouts: 6.11 us -> 2.46 us
    pallas_call x1, Pallas kernels: 36.3 us -> 42.4 us  [shards(): pl.pallas_call(functools.partial(kernel, rows), out_shape=jax.ShapeDtypeS...]
    unnamed x11 -> x1, local copies, waits for them, and re-layouts: 6.11 us -> 2.46 us
where the time goes in v4:
time: 45 us; the launch traced here: 44.8 us
  Pallas kernels  42.4 us (94%)
  local copies, waits for them, and re-layouts  2.46 us (5%)
    pallas_call x1, Pallas kernels, shards(): pl.pallas_call(functools.partial(kernel, rows), out_shape=jax.ShapeDtypeS...  42.4 us
    unnamed x1, local copies, waits for them, and re-layouts  2.46 us

profile of v4, /device:TPU:0, one launch (start us, length us, event | category | flops | bytes accessed | tf_op | source)
XLA Modules:
  0.0 44.8 jit_solution(2813250412062468677)
XLA Ops:
  0.0 42.4 %shard_map.55 = f32[2560,128]{1,0:T(8,128)} custom-call(f32[2560,128]{1,0:T(8,128)} %bitcast.6, bf16[4,320,320]{2,1,0:T(8,128)(2,1)} %table_in.1, bf16[960,320]{1,0:T(8,128)(2,1)} %bitcast.7, s32[8,128]{1,0:T(8,128)} %bitcast.9, s32[6,8,128]{2,1,0:T(8,128)} %bitcast.8), custom_call_target="tpu_custom_call" | custom-call | tf_op jit(solution)/shard_map/pallas_call | solution.py:363
  42.4 2.5 %copy.7 = f32[1,320,8,128]{3,2,1,0:T(8,128)} copy(f32[1,320,8,128]{3,2,1,0:T(8,128)} %bitcast.5) | data formatting | bytes 2621440

commit v5 on v4

--- a/solution.py
+++ b/solution.py
@@ -16,6 +16,7 @@
 HALVES = 2 * SWEEPS
 LANES = 128
 WIDE = 256
+DEPTH = 1024
 GROUP = 2
 MESH = pl.DeviceIdType.MESH
 F32 = jnp.float32
@@ -119,8 +120,10 @@
     pl.semaphore_wait(barrier, total)
 
     def lay_out_coupling():
-        tall_ref[: KC * 6 * TRACE, :BLOCK] = coupling_ref[...]
-        wide_ref[...] = jnp.transpose(tall_ref[...])[:BLOCK, : KC * 6 * TRACE]
+        filled = KC * 6 * TRACE
+        tall_ref[:filled, :BLOCK] = coupling_ref[...]
+        tall_ref[filled:, :BLOCK] = jnp.zeros((DEPTH - filled, BLOCK), BF16)
+        wide_ref[...] = jnp.transpose(tall_ref[...])[:BLOCK]
 
     lane = lax.broadcasted_iota(jnp.int32, (TRACE, LANES), 1)
     flip = lax.rem(places["cx"][0], 2)
@@ -373,12 +376,12 @@
             pltpu.VMEM((6, rows, LANES), jnp.int32),
             pltpu.SemaphoreType.DMA((5,)),
             pltpu.VMEM((BLOCK, KD * BLOCK), BF16),
-            pltpu.VMEM((8 * LANES, 3 * LANES), BF16),
-            pltpu.VMEM((BLOCK, inputs), BF16),
+            pltpu.VMEM((DEPTH, 3 * LANES), BF16),
+            pltpu.VMEM((BLOCK, DEPTH), BF16),
             pltpu.VMEM((rows, BLOCK, LANES), F32),
             pltpu.VMEM((GROUP, BLOCK, LANES), BF16),
             pltpu.VMEM((GROUP, 2, TRACE, LANES), F32),
-            pltpu.VMEM((groups, inputs, columns), BF16),
+            pltpu.VMEM((groups, DEPTH, columns), BF16),
             pltpu.VMEM((KD * BLOCK, columns), BF16),
             pltpu.VMEM((HALVES, groups, GROUP, TRACE, LANES), BF16),
             pltpu.VMEM((HALVES, groups, GROUP, TRACE, LANES), BF16),

time: 45 us -> 45 us (level)
  no operation moved by 1% of the time
where the time goes in v5:
time: 45 us; the launch traced here: 44.8 us
  Pallas kernels  42.4 us (94%)
  local copies, waits for them, and re-layouts  2.46 us (5%)
    pallas_call x1, Pallas kernels, shards(): pl.pallas_call(functools.partial(kernel, rows), out_shape=jax.ShapeDtypeS...  42.4 us
    unnamed x1, local copies, waits for them, and re-layouts  2.46 us

profile of v5, /device:TPU:0, one launch (start us, length us, event | category | flops | bytes accessed | tf_op | source)
XLA Modules:
  0.0 44.8 jit_solution(7010605696442377869)
XLA Ops:
  0.0 42.4 %shard_map.55 = f32[2560,128]{1,0:T(8,128)} custom-call(f32[2560,128]{1,0:T(8,128)} %bitcast.6, bf16[4,320,320]{2,1,0:T(8,128)(2,1)} %table_in.1, bf16[960,320]{1,0:T(8,128)(2,1)} %bitcast.7, s32[8,128]{1,0:T(8,128)} %bitcast.9, s32[6,8,128]{2,1,0:T(8,128)} %bitcast.8), custom_call_target="tpu_custom_call" | custom-call | tf_op jit(solution)/shard_map/pallas_call | solution.py:366
  42.4 2.5 %copy.7 = f32[1,320,8,128]{3,2,1,0:T(8,128)} copy(f32[1,320,8,128]{3,2,1,0:T(8,128)} %bitcast.5) | data formatting | bytes 2621440
